TPU v7x, 32 devices: a whole 2x2x4 slice. The times are simulated.
32 devices in a mesh: parts: 2 (over x), wall: 16 (over z, y, core).
Axes of the slice: x: 2, y: 2, z: 4, core: 2. Of those that a mesh axis runs over, the one named last changes fastest.
Arguments:
- displacement: float32 [3, 524288], P(None, ('parts', 'wall')), parts along dimension 1, may hold values from -6 to 6
- velocity: float32 [3, 524288], P(None, ('parts', 'wall')), parts along dimension 1, may hold values from -6 to 6
- send_list: int32 [32, 16, 64], P(('parts', 'wall')), parts along dimension 0, may hold values from 0 to 16383, as said below
- arrive_list: int32 [32, 16, 64], P(('parts', 'wall')), parts along dimension 0, may hold values from 0 to 16383, as said below
- recv_count: int32 [32, 16], P(('parts', 'wall')), parts along dimension 0, may hold values from 0 to 64, as said below
- horizon_blocks: int32 [4096, 27], P(('parts', 'wall')), parts along dimension 0, may hold values from 0 to 2047, as said below
- bond_intact: int32 [4096, 27, 128], P(('parts', 'wall')), parts along dimension 0, may hold values 0 or 1
- modulus: float32 [524288], P(('parts', 'wall')), parts along dimension 0, may hold values from 0.5 to 2
- bond_weight: bfloat16 [27, 128, 128], replicated, may hold values from -0.109375 to 0.109375
Outputs:
- new_displacement: float32 [3, 524288], P(None, ('parts', 'wall')), parts along dimension 1
- new_velocity: float32 [3, 524288], P(None, ('parts', 'wall')), parts along dimension 1
There are 2 independent parts, one for each index of `parts`. A program takes and returns all parts, laid end to end along the dimension named above; an argument that names none is the same for every part. Nothing has to cross between parts.
Inputs may be any that keep to these rules, and one draw needn't show every extreme that they name: For c < recv_count[d, s], send_list[s, d, c] is the local index on owner s of a node handed to owner d; the nodes that s hands away are distinct, and every owner hands away as many nodes as it receives. Other slots hold 0. For c < recv_count[d, s], arrive_list[d, s, c] is the local index on owner d where the c-th node from s lands; over all s and c these are exactly the local indices that d hands away, each once. Other slots hold 0. recv_count[d, s] is 0 for s = d and at least 1 otherwise; at most 64 nodes go from one owner to one other owner, and that many do on some pair in every draw. `horizon_blocks`: block b lies in layer b // 64; every block listed for b lies in the same layer, the layer before or the layer after.
All inputs are finite; a program needn't handle non-finite values. No bound on the sum of `bond_intact` on one device may be relied on, other than what follows from the above.
Results may differ from a plain program's by a relative error of at most 0.0011.
Values may be sent and summed in bfloat16 or wider, within the bound.
A program may use at most 64 MiB of HBM per device.

v0:
```python
import functools
import math

import jax
import jax.numpy as jnp
from jax import lax
from jax.experimental import pallas as pl
from jax.experimental.pallas import tpu as pltpu
from jax.sharding import PartitionSpec as P

SUBSTEPS = 2
LAYER = 64
PEER_BATCH = 16
TIME_STEP = 0.25
MESH = pl.DeviceIdType.MESH
F32 = jnp.float32
BF16 = jnp.bfloat16


def force_kernel(
    blocks,
    width,
    nnz,
    peers,
    send_hbm,
    arrive_hbm,
    count_hbm,
    hor_hbm,
    bonds_hbm,
    mod_hbm,
    weight_hbm,
    pos_hbm,
    vel_hbm,
    pos_ref,
    vel_ref,
    send_ref,
    arrive_ref,
    count_ref,
    hor_ref,
    mod_ref,
    weight_ref,
    pos_raw,
    vel_raw,
    pos_in,
    vel_in,
    out_buf,
    in_buf,
    spread_ref,
    landed_ref,
    raw_ref,
    intact_ref,
    wt_ref,
    onehot_ref,
    ext_ref,
    picked_ref,
    stiff_ref,
    acc_ref,
    stretch_ref,
    soften_ref,
    send_sem,
    recv_sem,
    node_send_sem,
    node_recv_sem,
    fetch_sem,
):
    me = lax.axis_index("wall")
    count = lax.axis_size("wall")
    reach = 3 * LAYER
    slots = 2 * (SUBSTEPS + 1)
    has_left = me > 0
    has_right = me < count - 1
    left = lax.rem(me + count - 1, count)
    right = lax.rem(me + 1, count)

    nodes = blocks * width
    capacity = send_ref.shape[1]
    shift = width.bit_length() - 1
    batch = math.gcd(PEER_BATCH, peers)
    lane_count = batch * capacity

    pairs = [(send_hbm.at[0], send_ref)]
    pairs += [(pos_hbm, pos_raw), (vel_hbm, vel_raw)]
    early = len(pairs)
    pairs += [(hor_hbm, hor_ref), (weight_hbm, weight_ref), (bonds_hbm, raw_ref)]
    pairs += [(arrive_hbm.at[0], arrive_ref), (count_hbm, count_ref), (mod_hbm, mod_ref)]
    fetches = [pltpu.make_async_copy(pair[0], pair[1], fetch_sem.at[i]) for i, pair in enumerate(pairs)]
    for fetch in fetches:
        fetch.start()

    barrier = pltpu.get_barrier_semaphore()

    def greet(step, carry):
        pl.semaphore_signal(
            barrier, inc=1, device_id={"wall": lax.rem(me + step, count)}, device_id_type=MESH
        )
        return carry

    lax.fori_loop(1, peers, greet, 0)

    def split(value):
        high = value.astype(BF16)
        low = (value - high.astype(F32)).astype(BF16)
        return high, low

    for fetch in fetches[:early]:
        fetch.wait()
    for row in range(3):
        pos_in[row] = pos_raw[:, row, :]
        vel_in[row] = vel_raw[:, row, :]
    state = [pos_in, pos_in, pos_in, vel_in, vel_in, vel_in]

    def gather_batch(step, carry):
        rows = send_ref[pl.ds(step * batch, batch), :]
        index = jnp.concatenate([rows[i : i + 1, :] for i in range(batch)], axis=1)
        picked_rows = []
        tile = 256 if lane_count % 256 == 0 else lane_count
        splits = [jnp.concatenate(split(state[row][row % 3]), axis=1) for row in range(6)]
        for start in range(0, lane_count, tile):
            part = index[:, start : start + tile]
            of_node = lax.broadcasted_iota(jnp.int32, (width, tile), 0) == (part & (width - 1))
            of_block = lax.broadcasted_iota(jnp.int32, (blocks, tile), 0) == (part >> shift)
            column = jnp.where(of_node, 1.0, 0.0).astype(BF16)
            column = jnp.concatenate([column, column], axis=0)
            values = []
            for row in range(6):
                found = jnp.dot(splits[row], column, preferred_element_type=F32)
                values.append(jnp.sum(jnp.where(of_block, found, 0.0), axis=0, keepdims=True))
            picked_rows.append(jnp.concatenate(values, axis=0))
        picked = jnp.concatenate(picked_rows, axis=1)
        for i in range(batch):
            out_buf[step * batch + i, 0:6, 0:capacity] = picked[:, i * capacity : (i + 1) * capacity]
        return carry

    lax.fori_loop(0, peers // batch, gather_batch, 0)
    in_buf[me, :, :] = jnp.zeros(in_buf.shape[1:], F32)
    pl.semaphore_wait(barrier, peers - 1)

    def node_copy(step):
        peer = lax.rem(me + step, count)
        return pltpu.make_async_remote_copy(
            src_ref=out_buf.at[peer],
            dst_ref=in_buf.at[me],
            send_sem=node_send_sem.at[peer],
            recv_sem=node_recv_sem.at[me],
            device_id={"wall": peer},
            device_id_type=MESH,
        )

    def node_arrival(step):
        peer = lax.rem(me + step, count)
        return pltpu.make_async_remote_copy(
            src_ref=out_buf.at[peer],
            dst_ref=in_buf.at[peer],
            send_sem=node_send_sem.at[peer],
            recv_sem=node_recv_sem.at[peer],
            device_id={"wall": peer},
            device_id_type=MESH,
        )

    def start_nodes(step, carry):
        node_copy(step).start()
        return carry

    lax.fori_loop(1, peers, start_nodes, 0)

    lanes = lax.broadcasted_iota(jnp.int32, (LAYER, reach), 1)
    fetches[early].wait()
    padding = jnp.zeros((-nnz % 8, blocks), jnp.int32)
    horizon = jnp.transpose(jnp.concatenate([hor_ref[...], padding], axis=0))
    for half in range(2):
        local = horizon[half * LAYER : (half + 1) * LAYER] - (me * blocks - LAYER + half * LAYER)
        for j in range(nnz):
            hit = local[:, j : j + 1] == lanes
            onehot_ref[half, pl.ds(j * LAYER, LAYER), :] = jnp.where(hit, 1.0, 0.0).astype(BF16)

    for fetch in fetches[early + 1 :]:
        fetch.wait()
    stiff = jnp.zeros((blocks, width), F32)
    ones = jnp.ones((16, width), BF16)
    for j in range(nnz):
        weight = jnp.transpose(weight_ref[j])
        wt_ref[j] = weight
        totals = jnp.dot(ones, weight, preferred_element_type=F32)[0:1, :]
        intact = raw_ref[j].astype(F32)
        intact_ref[j] = intact
        stiff = stiff + intact * totals
    stiff_ref[...] = stiff

    def halo_copy(slot, half, rows):
        wide = rows * width
        if half == 0:
            source = ext_ref.at[slot, pl.ds(LAYER, LAYER), pl.ds(0, wide)]
            target = ext_ref.at[slot, pl.ds(3 * LAYER, LAYER), pl.ds(0, wide)]
            device = left
        else:
            source = ext_ref.at[slot, pl.ds(2 * LAYER, LAYER), pl.ds(0, wide)]
            target = ext_ref.at[slot, pl.ds(0, LAYER), pl.ds(0, wide)]
            device = right
        return pltpu.make_async_remote_copy(
            src_ref=source,
            dst_ref=target,
            send_sem=send_sem.at[slot, half],
            recv_sem=recv_sem.at[slot, 1 - half],
            device_id={"wall": device},
            device_id_type=MESH,
        )

    def exists(half):
        return has_left if half == 0 else has_right

    def send(slot, half, rows):
        @pl.when(exists(half))
        def _():
            halo_copy(slot, half, rows).start()

    def wait_halo(slot, half, rows):
        @pl.when(exists(half))
        def _():
            halo_copy(slot, 1 - half, rows).wait_recv()

    def own(half):
        return pl.ds(half * LAYER, LAYER)

    def put(slot, half, row, value):
        ext_ref[slot, pl.ds(LAYER + half * LAYER, LAYER), pl.ds(row * width, width)] = value

    def get(slot, half, row):
        return ext_ref[slot, pl.ds(LAYER + half * LAYER, LAYER), pl.ds(row * width, width)].astype(F32)

    @pl.when(jnp.logical_not(has_left))
    def _():
        for slot in range(slots):
            ext_ref[slot, pl.ds(0, LAYER), :] = jnp.zeros((LAYER, 4 * width), BF16)

    @pl.when(jnp.logical_not(has_right))
    def _():
        for slot in range(slots):
            ext_ref[slot, pl.ds(3 * LAYER, LAYER), :] = jnp.zeros((LAYER, 4 * width), BF16)

    def finish_nodes(step, carry):
        node_arrival(step).wait()
        return carry

    lax.fori_loop(1, peers, finish_nodes, 0)

    landed_ref[...] = jnp.zeros(landed_ref.shape, F32)

    def scatter_batch(step, carry):
        rows = arrive_ref[pl.ds(step * batch, batch), :]
        slot_ids = lax.broadcasted_iota(jnp.int32, (1, capacity), 1)
        index = jnp.concatenate(
            [
                jnp.where(slot_ids < count_ref[0, step * batch + i], rows[i : i + 1, :], nodes)
                for i in range(batch)
            ],
            axis=1,
        )
        values = jnp.concatenate(
            [in_buf[step * batch + i][0:6, 0:capacity] for i in range(batch)], axis=1
        )
        high, low = split(values)
        parts = [high.astype(F32), low.astype(F32)]
        of_node = lax.broadcasted_iota(jnp.int32, (width, lane_count), 0) == (index & (width - 1))
        of_block = lax.broadcasted_iota(jnp.int32, (blocks, lane_count), 0) == (index >> shift)
        column = jnp.where(of_node, 1.0, 0.0).astype(BF16)
        for row in range(6):
            for k in range(2):
                spread_ref[pl.ds((2 * row + k) * blocks, blocks), :] = jnp.where(
                    of_block, parts[k][row : row + 1, :], 0.0
                ).astype(BF16)
        spread_ref[pl.ds(12 * blocks, blocks), :] = jnp.where(of_block, 1.0, 0.0).astype(BF16)
        landed_ref[...] = landed_ref[...] + lax.dot_general(
            spread_ref[...], column, (((1,), (1,)), ((), ())), preferred_element_type=F32
        )
        return carry

    lax.fori_loop(0, peers // batch, scatter_batch, 0)

    for half in (0, 1):
        hit = landed_ref[pl.ds(12 * blocks + half * LAYER, LAYER), :] > 0.5
        for row in range(6):
            high = landed_ref[pl.ds(2 * row * blocks + half * LAYER, LAYER), :]
            low = landed_ref[pl.ds((2 * row + 1) * blocks + half * LAYER, LAYER), :]
            value = jnp.where(hit, high + low, state[row][row % 3, own(half), :])
            if row < 3:
                pos_ref[row, own(half), :] = value
                put(0, half, row, value.astype(BF16))
            else:
                vel_ref[row - 3, own(half), :] = value
        send(0, half, 3)

    group = 9 if nnz % 9 == 0 else nnz

    def contract(slot, rows, half):
        wide = rows * width
        source = ext_ref[slot, pl.ds(half * LAYER, reach), pl.ds(0, wide)]
        for start in range(0, nnz, group):
            part = pl.ds(start * LAYER, group * LAYER)
            picked_ref[part, pl.ds(0, wide)] = jnp.dot(
                onehot_ref[half, part, :], source, preferred_element_type=F32
            ).astype(BF16)
        sums = [jnp.zeros((LAYER, width), F32) for _ in range(rows)]
        for j in range(nnz):
            part = pl.ds(j * LAYER, LAYER)
            mask = intact_ref[j, own(half), :]
            stacked = jnp.concatenate(
                [picked_ref[part, pl.ds(row * width, width)] for row in range(rows)], axis=0
            )
            product = jnp.dot(stacked, wt_ref[j], preferred_element_type=F32)
            for row in range(rows):
                sums[row] = sums[row] + product[row * LAYER : (row + 1) * LAYER] * mask
        return sums

    def evaluation(t, carry):
        near, far = 2 * t, 2 * t + 1
        for half in (0, 1):
            wait_halo(near, half, 3)
            summed = contract(near, 3, half)
            scaling = mod_ref[own(half), :]
            stiffness = stiff_ref[own(half), :]
            rounded = [get(near, half, row) for row in range(3)]
            stretch = [scaling * (summed[row] - stiffness * rounded[row]) for row in range(3)]
            dilatation = (stretch[0] + stretch[1] + stretch[2]) / 3.0
            soften = 1.0 / (1.0 + dilatation * dilatation)
            soft_low = soften.astype(BF16)
            soft_wide = soft_low.astype(F32)
            for row in range(3):
                put(far, half, row, (soft_wide * rounded[row]).astype(BF16))
                stretch_ref[row, own(half), :] = stretch[row]
            put(far, half, 3, soft_low)
            soften_ref[own(half), :] = soften
            send(far, half, 4)
        for half in (1, 0):
            wait_halo(far, half, 4)
            paired = contract(far, 4, half)
            scaling = mod_ref[own(half), :]
            soften = soften_ref[own(half), :]
            for row in range(3):
                rounded = get(near, half, row)
                force = 0.5 * (
                    scaling * (paired[row] - rounded * paired[3]) + soften * stretch_ref[row, own(half), :]
                )

                @pl.when(t > 0)
                def _():
                    vel_ref[row, own(half), :] = vel_ref[row, own(half), :] + 0.5 * TIME_STEP * (
                        acc_ref[row, own(half), :] + force
                    )

                acc_ref[row, own(half), :] = force

            @pl.when(t < SUBSTEPS)
            def _():
                for row in range(3):
                    moved = (
                        pos_ref[row, own(half), :]
                        + TIME_STEP * vel_ref[row, own(half), :]
                        + 0.5 * TIME_STEP * TIME_STEP * acc_ref[row, own(half), :]
                    )
                    pos_ref[row, own(half), :] = moved
                    put(2 * t + 2, half, row, moved.astype(BF16))
                send(2 * t + 2, half, 3)

        return carry

    lax.fori_loop(0, SUBSTEPS + 1, evaluation, 0)

    for half in range(2):
        @pl.when(exists(half))
        def _():
            for slot in range(slots):
                halo_copy(slot, half, 3 if slot % 2 == 0 else 4).wait_send()


def shards(
    displacement,
    velocity,
    send_list,
    arrive_list,
    recv_count,
    horizon_blocks,
    bond_intact,
    modulus,
    bond_weight,
):
    node_count = displacement.shape[1]
    blocks, nnz, width = bond_intact.shape
    peers, capacity = send_list.shape[1:]
    lane_count = math.gcd(PEER_BATCH, peers) * capacity
    slots = 2 * (SUBSTEPS + 1)
    vmem = pl.BlockSpec(memory_space=pltpu.VMEM)
    hbm = pl.BlockSpec(memory_space=pltpu.HBM)
    shape = jax.ShapeDtypeStruct((3, blocks, width), F32)
    final_position, final_speed = pl.pallas_call(
        functools.partial(force_kernel, blocks, width, nnz, peers),
        out_shape=(shape, shape),
        in_specs=[hbm] * 9,
        out_specs=(vmem, vmem),
        scratch_shapes=[
            pltpu.VMEM((peers, capacity), jnp.int32),
            pltpu.VMEM((peers, capacity), jnp.int32),
            pltpu.SMEM((1, peers), jnp.int32),
            pltpu.VMEM((nnz, blocks), jnp.int32),
            pltpu.VMEM((blocks, width), F32),
            pltpu.VMEM((nnz, width, width), BF16),
            pltpu.VMEM((blocks, 3, width), F32),
            pltpu.VMEM((blocks, 3, width), F32),
            pltpu.VMEM((3, blocks, width), F32),
            pltpu.VMEM((3, blocks, width), F32),
            pltpu.VMEM((peers, 8, 128 * pl.cdiv(capacity, 128)), F32),
            pltpu.VMEM((peers, 8, 128 * pl.cdiv(capacity, 128)), F32),
            pltpu.VMEM((13 * blocks, lane_count), BF16),
            pltpu.VMEM((13 * blocks, width), F32),
            pltpu.VMEM((nnz, blocks, width), jnp.int32),
            pltpu.VMEM((nnz, blocks, width), F32),
            pltpu.VMEM((nnz, width, width), BF16),
            pltpu.VMEM((2, nnz * LAYER, 3 * LAYER), BF16),
            pltpu.VMEM((slots, 4 * LAYER, 4 * width), BF16),
            pltpu.VMEM((nnz * LAYER, 4 * width), BF16),
            pltpu.VMEM((blocks, width), F32),
            pltpu.VMEM((3, blocks, width), F32),
            pltpu.VMEM((3, blocks, width), F32),
            pltpu.VMEM((blocks, width), F32),
            pltpu.SemaphoreType.DMA((slots, 2)),
            pltpu.SemaphoreType.DMA((slots, 2)),
            pltpu.SemaphoreType.DMA((peers,)),
            pltpu.SemaphoreType.DMA((peers,)),
            pltpu.SemaphoreType.DMA((9,)),
        ],
        compiler_params=pltpu.CompilerParams(
            collective_id=0, has_side_effects=True, vmem_limit_bytes=67043328
        ),
        name="forces",
    )(
        send_list,
        arrive_list,
        recv_count,
        jnp.transpose(horizon_blocks),
        jnp.transpose(bond_intact, (1, 0, 2)),
        modulus.reshape(blocks, width),
        bond_weight,
        jnp.transpose(displacement.reshape(3, blocks, width), (1, 0, 2)),
        jnp.transpose(velocity.reshape(3, blocks, width), (1, 0, 2)),
    )
    return (final_position.reshape(3, node_count), final_speed.reshape(3, node_count))


def solution(mesh):
    in_specs = (
        P(None, ("parts", "wall")),
        P(None, ("parts", "wall")),
        P(("parts", "wall"), None, None),
        P(("parts", "wall"), None, None),
        P(("parts", "wall"), None),
        P(("parts", "wall"), None),
        P(("parts", "wall"), None, None),
        P(("parts", "wall")),
        P(),
    )
    out_specs = (P(None, ("parts", "wall")), P(None, ("parts", "wall")))
    return jax.shard_map(shards, mesh=mesh, in_specs=in_specs, out_specs=out_specs, check_vma=False)
```

profile of v0, /device:TPU:5, one launch (start us, length us, event | category | flops | bytes accessed | tf_op | source)
XLA Modules:
  0.0 39.7 jit_solution(17990479511045602062)
XLA Ops:
  0.6 37.0 %forces.1 = (f32[3,128,128]{2,1,0:T(8,128)}, f32[3,128,128]{2,1,0:T(8,128)}) custom-call(s32[1,16,64]{2,1,0:T(8,128)} %send_hbm.1, s32[1,16,64]{2,1,0:T(8,128)} %arrive_hbm.1, s32[1,16]{1,0:T(1,128)} %count_hbm.1, s32[27,128]{1,0:T(8,128)} %bitcast.21, s32[27,128,128]{2,1,0:T(8,128)} %bitcast.15, f32[128,128]{1,0:T(8,128)} %bitcast.20, ...), custom_call_target="tpu_custom_call" | custom-call | tf_op jit(solution)/shard_map/forces/pallas_call | solution.py:394
  37.7 2.1 %copy_bitcast_fusion = (f32[3,16384]{1,0:T(4,128)}, f32[3,16384]{1,0:T(4,128)}) fusion(f32[1,3,128,128]{3,2,1,0:T(8,128)} %bitcast.19, f32[1,3,128,128]{3,2,1,0:T(8,128)} %bitcast.18), kind=kLoop, calls=%fused_computation | loop fusion | bytes 786432 | tf_op jit(solution)/shard_map/reshape | solution.py:445
where the time goes:
time: 40 us; the launch traced here: 39.7 us
  Pallas kernels  37 us (92%)
  local copies, waits for them, and re-layouts  2.08 us (5%)
  between operations  0.64 us (2%)
    pallas_call x1, Pallas kernels, shards(): pl.pallas_call(functools.partial(force_kernel, blocks, width, nnz, peers)...  37 us
    reshape x1, local copies, waits for them, and re-layouts, shards(): final_speed.reshape(3, node_count)  2.08 us

commit v1 on v0

--- a/solution.py
+++ b/solution.py
@@ -12,6 +12,7 @@
 LAYER = 64
 PEER_BATCH = 16
 TIME_STEP = 0.25
+VMEM_LIMIT = 66977792
 MESH = pl.DeviceIdType.MESH
 F32 = jnp.float32
 BF16 = jnp.bfloat16
@@ -31,8 +32,8 @@
     weight_hbm,
     pos_hbm,
     vel_hbm,
-    pos_ref,
-    vel_ref,
+    pos_out,
+    vel_out,
     send_ref,
     arrive_ref,
     count_ref,
@@ -62,6 +63,8 @@
     node_send_sem,
     node_recv_sem,
     fetch_sem,
+    pos_ref,
+    vel_ref,
 ):
     me = lax.axis_index("wall")
     count = lax.axis_size("wall")
@@ -365,11 +368,26 @@
 
     lax.fori_loop(0, SUBSTEPS + 1, evaluation, 0)
 
+    for row in range(3):
+        pos_out[:, row, :] = pos_ref[row]
+        vel_out[:, row, :] = vel_ref[row]
+
     for half in range(2):
         @pl.when(exists(half))
         def _():
             for slot in range(slots):
                 halo_copy(slot, half, 3 if slot % 2 == 0 else 4).wait_send()
+
+
+def store_kernel(pos_in, vel_in, pos_out, vel_out, sems):
+    copies = [
+        pltpu.make_async_copy(pos_in, pos_out, sems.at[0]),
+        pltpu.make_async_copy(vel_in, vel_out, sems.at[1]),
+    ]
+    for copy in copies:
+        copy.start()
+    for copy in copies:
+        copy.wait()
 
 
 def shards(
@@ -390,10 +408,11 @@
     slots = 2 * (SUBSTEPS + 1)
     vmem = pl.BlockSpec(memory_space=pltpu.VMEM)
     hbm = pl.BlockSpec(memory_space=pltpu.HBM)
-    shape = jax.ShapeDtypeStruct((3, blocks, width), F32)
+    shape = jax.ShapeDtypeStruct((blocks, 3, width), F32)
+    spare = VMEM_LIMIT - 2 * 4 * blocks * 4 * width
     final_position, final_speed = pl.pallas_call(
         functools.partial(force_kernel, blocks, width, nnz, peers),
-        out_shape=(shape, shape),
+        out_shape=(pltpu.VMEM(shape.shape, F32), pltpu.VMEM(shape.shape, F32)),
         in_specs=[hbm] * 9,
         out_specs=(vmem, vmem),
         scratch_shapes=[
@@ -426,9 +445,11 @@
             pltpu.SemaphoreType.DMA((peers,)),
             pltpu.SemaphoreType.DMA((peers,)),
             pltpu.SemaphoreType.DMA((9,)),
+            pltpu.VMEM((3, blocks, width), F32),
+            pltpu.VMEM((3, blocks, width), F32),
         ],
         compiler_params=pltpu.CompilerParams(
-            collective_id=0, has_side_effects=True, vmem_limit_bytes=67043328
+            collective_id=0, has_side_effects=True, vmem_limit_bytes=spare
         ),
         name="forces",
     )(
@@ -442,7 +463,16 @@
         jnp.transpose(displacement.reshape(3, blocks, width), (1, 0, 2)),
         jnp.transpose(velocity.reshape(3, blocks, width), (1, 0, 2)),
     )
-    return (final_position.reshape(3, node_count), final_speed.reshape(3, node_count))
+    final_position, final_speed = pl.pallas_call(
+        store_kernel,
+        out_shape=(shape, shape),
+        in_specs=[pl.BlockSpec(memory_space=pl.ANY)] * 2,
+        out_specs=(hbm, hbm),
+        scratch_shapes=[pltpu.SemaphoreType.DMA((2,))],
+        compiler_params=pltpu.CompilerParams(vmem_limit_bytes=1048576),
+        name="store",
+    )(final_position, final_speed)
+    return tuple(jnp.transpose(x, (1, 0, 2)).reshape(3, node_count) for x in (final_position, final_speed))
 
 
 def solution(mesh):

time: 40 us -> 38.1 us (0.953)
  local copies, waits for them, and re-layouts: 2.08 us -> 0 us
    reshape x1 -> x0, local copies, waits for them, and re-layouts: 2.08 us -> none  [shards(): final_speed.reshape(3, node_count)]
    pallas_call x0 -> x1, Pallas kernels: none -> 0.76 us  [shards(): pl.pallas_call(store_kernel, out_shape=(shape, shape), in_specs=[pl.Block...]
    pallas_call x1, Pallas kernels: 37 us -> 36.5 us  [shards(): pl.pallas_call(functools.partial(force_kernel, blocks, width, nnz, peers)...]
where the time goes in v1:
time: 38.1 us; the launch traced here: 37.9 us
  Pallas kernels  37.3 us (98%)
  between operations  0.64 us (2%)
    pallas_call x1, Pallas kernels, shards(): pl.pallas_call(functools.partial(force_kernel, blocks, width, nnz, peers)...  36.5 us

profile of v1, /device:TPU:5, one launch (start us, length us, event | category | flops | bytes accessed | tf_op | source)
XLA Modules:
  0.0 37.9 jit_solution(14539242948142874158)
XLA Ops:
  0.6 36.5 %forces.1 = (f32[128,3,128]{2,1,0:T(4,128)S(1)}, f32[128,3,128]{2,1,0:T(4,128)S(1)}) custom-call(s32[1,16,64]{2,1,0:T(8,128)} %send_hbm.1, s32[1,16,64]{2,1,0:T(8,128)} %arrive_hbm.1, s32[1,16]{1,0:T(1,128)} %count_hbm.1, s32[27,128]{1,0:T(8,128)} %bitcast.19, s32[27,128,128]{2,1,0:T(8,128)} %bitcast.15, f32[128,128]{1,0:T(8,128)} %bitcast.18, ...), custom_call_target="tpu_custom_call" | custom-call | tf_op jit(solution)/shard_map/forces/pallas_call | solution.py:413
  37.1 0.8 %store.1 = (f32[128,3,128]{2,1,0:T(4,128)}, f32[128,3,128]{2,1,0:T(4,128)}) custom-call(f32[128,3,128]{2,1,0:T(4,128)S(1)} %get-tuple-element.6.pos_in, f32[128,3,128]{2,1,0:T(4,128)S(1)} %get-tuple-element.7.vel_in), custom_call_target="tpu_custom_call" | custom-call | tf_op jit(solution)/shard_map/store/pallas_call | solution.py:466

commit v2 on v1

v2 whole, which is shorter than its diff:
```python
import functools
import math

import jax
import jax.numpy as jnp
from jax import lax
from jax.experimental import pallas as pl
from jax.experimental.pallas import tpu as pltpu
from jax.sharding import PartitionSpec as P

SUBSTEPS = 2
LAYER = 64
PEER_BATCH = 16
TIME_STEP = 0.25
VMEM_LIMIT = 66977792
MESH = pl.DeviceIdType.MESH
F32 = jnp.float32
BF16 = jnp.bfloat16


def force_kernel(
    blocks,
    width,
    nnz,
    peers,
    send_hbm,
    arrive_hbm,
    count_hbm,
    hor_hbm,
    bonds_hbm,
    mod_hbm,
    weight_hbm,
    pos_hbm,
    vel_hbm,
    pos_out,
    vel_out,
    send_ref,
    arrive_ref,
    count_ref,
    hor_ref,
    mod_ref,
    weight_ref,
    pos_raw,
    vel_raw,
    pos_in,
    vel_in,
    out_buf,
    in_buf,
    index_ref,
    node_ref,
    block_ref,
    hit_ref,
    spread_ref,
    landed_ref,
    ghost_spread_ref,
    ghost_landed_ref,
    raw_ref,
    intact_ref,
    wt_ref,
    onehot_ref,
    ext_ref,
    picked_ref,
    stiff_ref,
    stretch_ref,
    soften_ref,
    pos_ref,
    vel_ref,
    send_sem,
    recv_sem,
    index_send_sem,
    index_recv_sem,
    node_send_sem,
    node_recv_sem,
    fetch_sem,
):
    me = lax.axis_index("wall")
    count = lax.axis_size("wall")
    reach = 3 * LAYER
    slots = 2 * (SUBSTEPS + 1)
    slow = lax.rem(me, 2)
    fast = 1 - slow

    nodes = blocks * width
    capacity = send_ref.shape[1]
    shift = width.bit_length() - 1
    batch = math.gcd(PEER_BATCH, peers)
    lane_count = batch * capacity

    pairs = [(send_hbm.at[0], send_ref)]
    pairs += [(pos_hbm, pos_raw), (vel_hbm, vel_raw)]
    early = len(pairs)
    pairs += [(arrive_hbm.at[0], arrive_ref), (count_hbm, count_ref)]
    listed = len(pairs)
    pairs += [(hor_hbm, hor_ref), (weight_hbm, weight_ref), (bonds_hbm, raw_ref), (mod_hbm, mod_ref)]
    fetches = [pltpu.make_async_copy(pair[0], pair[1], fetch_sem.at[i]) for i, pair in enumerate(pairs)]
    for fetch in fetches:
        fetch.start()

    barrier = pltpu.get_barrier_semaphore()

    def greet(step, carry):
        pl.semaphore_signal(
            barrier, inc=1, device_id={"wall": lax.rem(me + step, count)}, device_id_type=MESH
        )
        return carry

    lax.fori_loop(1, peers, greet, 0)

    def split(value):
        high = value.astype(BF16)
        low = (value - high.astype(F32)).astype(BF16)
        return high, low

    def neighbour(half):
        return lax.rem(me + count - 1 + 2 * half, count)

    def exists(half):
        there = me - 1 + 2 * half
        return jnp.logical_and(there >= 0, there < count)

    def own(half):
        return pl.ds(half * LAYER if isinstance(half, int) else pl.multiple_of(half * LAYER, LAYER), LAYER)

    def held(half):
        start = LAYER + half * LAYER
        return pl.ds(start if isinstance(half, int) else pl.multiple_of(start, LAYER), LAYER)

    def halo_copy(slot, half, part, lanes):
        start = 3 * LAYER * (1 - half)
        target = pl.ds(start if isinstance(half, int) else pl.multiple_of(start, LAYER), LAYER)
        return pltpu.make_async_remote_copy(
            src_ref=ext_ref.at[slot, held(half), lanes],
            dst_ref=ext_ref.at[slot, target, lanes],
            send_sem=send_sem.at[slot, half, part],
            recv_sem=recv_sem.at[slot, 1 - half, part],
            device_id={"wall": neighbour(half)},
            device_id_type=MESH,
        )

    def lanes_of(first, rows):
        return pl.ds(first * width, rows * width)

    def send(slot, half, part, lanes):
        @pl.when(exists(half))
        def _():
            halo_copy(slot, half, part, lanes).start()

    def wait_halo(slot, half, part, lanes):
        @pl.when(exists(half))
        def _():
            halo_copy(slot, 1 - half, part, lanes).wait_recv()

    def wait_sent(slot, half, part, lanes):
        @pl.when(exists(half))
        def _():
            halo_copy(slot, half, part, lanes).wait_send()

    def put(slot, half, column, value):
        ext_ref[slot, held(half), lanes_of(column, 1)] = value

    def get(slot, half, column):
        return ext_ref[slot, held(half), lanes_of(column, 1)].astype(F32)

    def index_copy(half):
        return pltpu.make_async_remote_copy(
            src_ref=index_ref.at[1],
            dst_ref=index_ref.at[2 - 2 * half],
            send_sem=index_send_sem.at[half],
            recv_sem=index_recv_sem.at[1 - half],
            device_id={"wall": neighbour(half)},
            device_id_type=MESH,
        )

    out_buf[...] = jnp.zeros(out_buf.shape, F32)
    for fetch in fetches[:early]:
        fetch.wait()
    for row in range(3):
        pos_in[row] = pos_raw[:, row, :]
        vel_in[row] = vel_raw[:, row, :]
    state = [pos_in, pos_in, pos_in, vel_in, vel_in, vel_in]

    def gather_batch(step, carry):
        rows = send_ref[pl.ds(step * batch, batch), :]
        index = jnp.concatenate([rows[i : i + 1, :] for i in range(batch)], axis=1)
        placed_rows = []
        speed_rows = []
        tile = 256 if lane_count % 256 == 0 else lane_count
        splits = [jnp.concatenate(split(state[row][row % 3]), axis=1) for row in range(6)]
        for start in range(0, lane_count, tile):
            part = index[:, start : start + tile]
            of_node = lax.broadcasted_iota(jnp.int32, (width, tile), 0) == (part & (width - 1))
            of_block = lax.broadcasted_iota(jnp.int32, (blocks, tile), 0) == (part >> shift)
            column = jnp.where(of_node, 1.0, 0.0).astype(BF16)
            column = jnp.concatenate([column, column], axis=0)
            values = []
            for row in range(6):
                found = jnp.dot(splits[row], column, preferred_element_type=F32)
                values.append(jnp.sum(jnp.where(of_block, found, 0.0), axis=0, keepdims=True))
            placed_rows.append(jnp.concatenate(values[:3] + values[:3], axis=0))
            speed_rows.append(jnp.concatenate(values[3:], axis=0))
        placed = jnp.concatenate(placed_rows, axis=1)
        speeds = jnp.concatenate(speed_rows, axis=1)
        for i in range(batch):
            peer = step * batch + i
            mine = slice(i * capacity, (i + 1) * capacity)
            out_buf[peer + 1, 0:3, 0:capacity] = placed[0:3, mine]
            out_buf[peer + 1, 0:3, capacity : 2 * capacity] = speeds[:, mine]
            out_buf[peer + 2, 3:6, 0:capacity] = placed[3:6, mine]
            out_buf[peer, 3:6, capacity : 2 * capacity] = placed[3:6, mine]
        return carry

    lax.fori_loop(0, peers // batch, gather_batch, 0)
    in_buf[me, 0:6, :] = out_buf[me + 1, 0:6, :]
    pl.semaphore_wait(barrier, peers - 1)

    def node_copy(step):
        peer = lax.rem(me + step, count)
        return pltpu.make_async_remote_copy(
            src_ref=out_buf.at[peer + 1, pl.ds(0, 6), :],
            dst_ref=in_buf.at[me, pl.ds(0, 6), :],
            send_sem=node_send_sem.at[peer],
            recv_sem=node_recv_sem.at[me],
            device_id={"wall": peer},
            device_id_type=MESH,
        )

    def node_arrival(step):
        peer = lax.rem(me + step, count)
        return pltpu.make_async_remote_copy(
            src_ref=out_buf.at[peer + 1, pl.ds(0, 6), :],
            dst_ref=in_buf.at[peer, pl.ds(0, 6), :],
            send_sem=node_send_sem.at[peer],
            recv_sem=node_recv_sem.at[peer],
            device_id={"wall": peer},
            device_id_type=MESH,
        )

    def start_nodes(step, carry):
        node_copy(step).start()
        return carry

    lax.fori_loop(1, peers, start_nodes, 0)

    for half in (0, 1):
        for row in range(3):
            put(0, half, row, pos_in[row, own(half), :].astype(BF16))
        send(0, half, 0, lanes_of(0, 3))

    for fetch in fetches[early:listed]:
        fetch.wait()

    def index_batch(step, carry):
        rows = arrive_ref[pl.ds(step * batch, batch), :]
        slot_ids = lax.broadcasted_iota(jnp.int32, (1, capacity), 1)
        index_ref[1, step] = jnp.concatenate(
            [
                jnp.where(slot_ids < count_ref[0, step * batch + i], rows[i : i + 1, :], nodes)
                for i in range(batch)
            ],
            axis=1,
        )
        return carry

    lax.fori_loop(0, peers // batch, index_batch, 0)
    for half in (0, 1):

        @pl.when(exists(half))
        def _():
            index_copy(half).start()

        @pl.when(jnp.logical_not(exists(half)))
        def _():
            index_ref[2 * half] = jnp.full(index_ref.shape[1:], nodes, jnp.int32)
            for slot in range(slots):
                ext_ref[slot, pl.ds(3 * LAYER * half, LAYER), :] = jnp.zeros((LAYER, 4 * width), BF16)

    lanes = lax.broadcasted_iota(jnp.int32, (LAYER, reach), 1)
    fetches[listed].wait()
    padding = jnp.zeros((-nnz % 8, blocks), jnp.int32)
    horizon = jnp.transpose(jnp.concatenate([hor_ref[...], padding], axis=0))
    for half in range(2):
        local = horizon[half * LAYER : (half + 1) * LAYER] - (me * blocks - LAYER + half * LAYER)
        for j in range(nnz):
            hit = local[:, j : j + 1] == lanes
            onehot_ref[half, pl.ds(j * LAYER, LAYER), :] = jnp.where(hit, 1.0, 0.0).astype(BF16)

    for fetch in fetches[listed + 1 :]:
        fetch.wait()
    stiff = jnp.zeros((blocks, width), F32)
    ones = jnp.ones((16, width), BF16)
    for j in range(nnz):
        weight = jnp.transpose(weight_ref[j])
        wt_ref[j] = weight
        totals = jnp.dot(ones, weight, preferred_element_type=F32)[0:1, :]
        intact = raw_ref[j].astype(F32)
        intact_ref[j] = intact
        stiff = stiff + intact * totals
    stiff_ref[...] = stiff

    for half in (0, 1):

        @pl.when(exists(half))
        def _():
            index_copy(1 - half).wait_recv()

    def mark_batch(step, carry):
        for which in range(3):
            index = index_ref[which, step]
            of_node = lax.broadcasted_iota(jnp.int32, (width, lane_count), 0) == (index & (width - 1))
            node_ref[which, step] = jnp.where(of_node, 1.0, 0.0).astype(BF16)
            depth = blocks if which == 1 else LAYER
            first = LAYER if which == 0 else 0
            of_block = lax.broadcasted_iota(jnp.int32, (depth, lane_count), 0) + first == (index >> shift)
            marks = jnp.where(of_block, 1.0, 0.0).astype(BF16)
            start = (blocks + LAYER, 0, blocks)[which]
            block_ref[step, pl.ds(start, depth), :] = marks
            hit_ref[pl.ds(start, depth), :] = hit_ref[pl.ds(start, depth), :] + lax.dot_general(
                marks, node_ref[which, step], (((1,), (1,)), ((), ())), preferred_element_type=F32
            )
        return carry

    hit_ref[...] = jnp.zeros(hit_ref.shape, F32)
    lax.fori_loop(0, peers // batch, mark_batch, 0)

    landed_ref[...] = jnp.zeros(landed_ref.shape, F32)
    ghost_landed_ref[...] = jnp.zeros(ghost_landed_ref.shape, F32)

    for half in (0, 1):
        wait_halo(0, half, 0, lanes_of(0, 3))
        wait_sent(0, half, 0, lanes_of(0, 3))

    def finish_nodes(step, carry):
        node_arrival(step).wait()
        return carry

    lax.fori_loop(1, peers, finish_nodes, 0)

    def scatter_batch(step, carry):
        bundles = [in_buf[step * batch + i, 0:6, :] for i in range(batch)]
        first = jnp.concatenate([bundle[:, 0:capacity] for bundle in bundles], axis=1)
        second = jnp.concatenate([bundle[:, capacity : 2 * capacity] for bundle in bundles], axis=1)
        marks = block_ref[step, pl.ds(0, blocks), :]
        for k, values in enumerate((first, second)):
            parts = split(values)
            for row in range(3):
                for low in range(2):
                    spread_ref[pl.ds((6 * k + 2 * row + low) * blocks, blocks), :] = (
                        marks * parts[low][row : row + 1, :]
                    )
                side = pl.ds(blocks + LAYER - k * LAYER, LAYER)
                ghost_spread_ref[k, pl.ds(row * LAYER, LAYER), :] = (
                    block_ref[step, side, :] * parts[0][3 + row : 4 + row, :]
                )
            ghost_landed_ref[k] = ghost_landed_ref[k] + lax.dot_general(
                ghost_spread_ref[k], node_ref[2 * k, step], (((1,), (1,)), ((), ())), preferred_element_type=F32
            )
        landed_ref[...] = landed_ref[...] + lax.dot_general(
            spread_ref[...], node_ref[1, step], (((1,), (1,)), ((), ())), preferred_element_type=F32
        )
        return carry

    lax.fori_loop(0, peers // batch, scatter_batch, 0)

    for k in (0, 1):
        hit = hit_ref[pl.ds(blocks + LAYER - k * LAYER, LAYER), :] > 0.5
        for row in range(3):
            where = (0, pl.ds(3 * LAYER * k, LAYER), lanes_of(row, 1))
            landed = ghost_landed_ref[k, pl.ds(row * LAYER, LAYER), :]
            ext_ref[where] = jnp.where(hit, landed, ext_ref[where].astype(F32)).astype(BF16)
    for half in (0, 1):
        hit = hit_ref[own(half), :] > 0.5
        for row in range(6):
            high = landed_ref[pl.ds(2 * row * blocks + half * LAYER, LAYER), :]
            low = landed_ref[pl.ds((2 * row + 1) * blocks + half * LAYER, LAYER), :]
            value = jnp.where(hit, high + low, state[row][row % 3, own(half), :])
            if row < 3:
                pos_ref[row, own(half), :] = value
                put(0, half, row, value.astype(BF16))
            else:
                vel_ref[row - 3, own(half), :] = value

    group = 9 if nnz % 9 == 0 else nnz

    def contract(slot, first, rows, half):
        wide = rows * width
        start = half * LAYER if isinstance(half, int) else pl.multiple_of(half * LAYER, LAYER)
        source = ext_ref[slot, pl.ds(start, reach), lanes_of(first, rows)]
        for begin in range(0, nnz, group):
            part = pl.ds(begin * LAYER, group * LAYER)
            picked_ref[part, lanes_of(first, rows)] = jnp.dot(
                onehot_ref[half, part, :], source, preferred_element_type=F32
            ).astype(BF16)
        sums = [jnp.zeros((LAYER, width), F32) for _ in range(rows)]
        for j in range(nnz):
            part = pl.ds(j * LAYER, LAYER)
            mask = intact_ref[j, own(half), :]
            stacked = jnp.concatenate(
                [picked_ref[part, lanes_of(first + row, 1)] for row in range(rows)], axis=0
            )
            product = jnp.dot(stacked, wt_ref[j], preferred_element_type=F32)
            for row in range(rows):
                sums[row] = sums[row] + product[row * LAYER : (row + 1) * LAYER] * mask
        return sums

    def near_parts(apart):
        return ((0, 1), (1, 2)) if apart else ((0, 3),)

    def far_parts(apart):
        return ((0, 2), (2, 2)) if apart else ((0, 4),)

    def stretching(t, half, apart, waits):
        near, far = 2 * t, 2 * t + 1
        summed = []
        for part, (first, rows) in enumerate(near_parts(apart)):
            if waits:
                wait_halo(near, half, part, lanes_of(first, rows))
            summed += contract(near, first, rows, half)
        scaling = mod_ref[own(half), :]
        stiffness = stiff_ref[own(half), :]
        rounded = [get(near, half, row) for row in range(3)]
        stretch = [scaling * (summed[row] - stiffness * rounded[row]) for row in range(3)]
        dilatation = (stretch[0] + stretch[1] + stretch[2]) / 3.0
        soften = 1.0 / (1.0 + dilatation * dilatation)
        soft_low = soften.astype(BF16)
        soft_wide = soft_low.astype(F32)
        put(far, half, 0, soft_low)
        for row in range(3):
            put(far, half, 1 + row, (soft_wide * rounded[row]).astype(BF16))
        for part, (first, rows) in enumerate(far_parts(apart)):
            send(far, half, part, lanes_of(first, rows))
        for row in range(3):
            stretch_ref[row, own(half), :] = stretch[row]
        soften_ref[own(half), :] = soften

    def pairing(t, half, apart, last):
        near, far = 2 * t, 2 * t + 1
        scaling = mod_ref[own(half), :]
        soften = soften_ref[own(half), :]
        kick = 0.5 * TIME_STEP if last else jnp.where(t == 0, 0.5 * TIME_STEP, TIME_STEP)
        paired = []
        for part, (first, rows) in enumerate(far_parts(apart)):
            wait_halo(far, half, part, lanes_of(first, rows))
            begin = max(len(paired) - 1, 0)
            paired += contract(far, first, rows, half)
            for row in range(begin, len(paired) - 1):
                rounded = get(near, half, row)
                force = 0.5 * (
                    scaling * (paired[1 + row] - rounded * paired[0]) + soften * stretch_ref[row, own(half), :]
                )
                speed = vel_ref[row, own(half), :] + kick * force
                if last:
                    vel_out[own(half), row, :] = speed
                else:
                    vel_ref[row, own(half), :] = speed
                    moved = pos_ref[row, own(half), :] + TIME_STEP * speed
                    pos_ref[row, own(half), :] = moved
                    put(near + 2, half, row, moved.astype(BF16))
            if not last:
                send(near + 2, half, part, lanes_of(*near_parts(apart)[part]))

    stretching(0, slow, True, False)
    stretching(0, fast, False, False)

    def substep(t, carry):
        pairing(t, fast, False, False)
        pairing(t, slow, True, False)
        stretching(t + 1, fast, False, True)
        stretching(t + 1, slow, True, True)
        return carry

    lax.fori_loop(0, SUBSTEPS, substep, 0)

    for row in range(3):
        pos_out[:, row, :] = pos_ref[row]
    pairing(SUBSTEPS, fast, False, True)
    pairing(SUBSTEPS, slow, True, True)

    for half in (0, 1):

        @pl.when(exists(half))
        def _():
            index_copy(half).wait_send()

    for slot in range(1, slots):
        for half, apart in ((fast, False), (slow, True)):
            parts = far_parts(apart) if slot % 2 else near_parts(apart)
            for part, (first, rows) in enumerate(parts):
                wait_sent(slot, half, part, lanes_of(first, rows))


def store_kernel(pos_in, vel_in, pos_out, vel_out, sems):
    copies = [
        pltpu.make_async_copy(pos_in, pos_out, sems.at[0]),
        pltpu.make_async_copy(vel_in, vel_out, sems.at[1]),
    ]
    for copy in copies:
        copy.start()
    for copy in copies:
        copy.wait()


def shards(
    displacement,
    velocity,
    send_list,
    arrive_list,
    recv_count,
    horizon_blocks,
    bond_intact,
    modulus,
    bond_weight,
):
    node_count = displacement.shape[1]
    blocks, nnz, width = bond_intact.shape
    peers, capacity = send_list.shape[1:]
    lane_count = math.gcd(PEER_BATCH, peers) * capacity
    batches = peers * capacity // lane_count
    bundle_width = 128 * pl.cdiv(2 * capacity, 128)
    slots = 2 * (SUBSTEPS + 1)
    vmem = pl.BlockSpec(memory_space=pltpu.VMEM)
    hbm = pl.BlockSpec(memory_space=pltpu.HBM)
    shape = jax.ShapeDtypeStruct((blocks, 3, width), F32)
    spare = VMEM_LIMIT - 2 * 4 * blocks * 4 * width
    final_position, final_speed = pl.pallas_call(
        functools.partial(force_kernel, blocks, width, nnz, peers),
        out_shape=(pltpu.VMEM(shape.shape, F32), pltpu.VMEM(shape.shape, F32)),
        in_specs=[hbm] * 9,
        out_specs=(vmem, vmem),
        scratch_shapes=[
            pltpu.VMEM((peers, capacity), jnp.int32),
            pltpu.VMEM((peers, capacity), jnp.int32),
            pltpu.SMEM((1, peers), jnp.int32),
            pltpu.VMEM((nnz, blocks), jnp.int32),
            pltpu.VMEM((blocks, width), F32),
            pltpu.VMEM((nnz, width, width), BF16),
            pltpu.VMEM((blocks, 3, width), F32),
            pltpu.VMEM((blocks, 3, width), F32),
            pltpu.VMEM((3, blocks, width), F32),
            pltpu.VMEM((3, blocks, width), F32),
            pltpu.VMEM((peers + 2, 8, bundle_width), F32),
            pltpu.VMEM((peers, 8, bundle_width), F32),
            pltpu.VMEM((3, batches, 1, lane_count), jnp.int32),
            pltpu.VMEM((3, batches, width, lane_count), BF16),
            pltpu.VMEM((batches, blocks + 2 * LAYER, lane_count), BF16),
            pltpu.VMEM((blocks + 2 * LAYER, width), F32),
            pltpu.VMEM((12 * blocks, lane_count), BF16),
            pltpu.VMEM((12 * blocks, width), F32),
            pltpu.VMEM((2, 3 * LAYER, lane_count), BF16),
            pltpu.VMEM((2, 3 * LAYER, width), F32),
            pltpu.VMEM((nnz, blocks, width), jnp.int32),
            pltpu.VMEM((nnz, blocks, width), F32),
            pltpu.VMEM((nnz, width, width), BF16),
            pltpu.VMEM((2, nnz * LAYER, 3 * LAYER), BF16),
            pltpu.VMEM((slots, 4 * LAYER, 4 * width), BF16),
            pltpu.VMEM((nnz * LAYER, 4 * width), BF16),
            pltpu.VMEM((blocks, width), F32),
            pltpu.VMEM((3, blocks, width), F32),
            pltpu.VMEM((blocks, width), F32),
            pltpu.VMEM((3, blocks, width), F32),
            pltpu.VMEM((3, blocks, width), F32),
            pltpu.SemaphoreType.DMA((slots, 2, 2)),
            pltpu.SemaphoreType.DMA((slots, 2, 2)),
            pltpu.SemaphoreType.DMA((2,)),
            pltpu.SemaphoreType.DMA((2,)),
            pltpu.SemaphoreType.DMA((peers,)),
            pltpu.SemaphoreType.DMA((peers,)),
            pltpu.SemaphoreType.DMA((9,)),
        ],
        compiler_params=pltpu.CompilerParams(
            collective_id=0, has_side_effects=True, vmem_limit_bytes=spare
        ),
        name="forces",
    )(
        send_list,
        arrive_list,
        recv_count,
        jnp.transpose(horizon_blocks),
        jnp.transpose(bond_intact, (1, 0, 2)),
        modulus.reshape(blocks, width),
        bond_weight,
        jnp.transpose(displacement.reshape(3, blocks, width), (1, 0, 2)),
        jnp.transpose(velocity.reshape(3, blocks, width), (1, 0, 2)),
    )
    final_position, final_speed = pl.pallas_call(
        store_kernel,
        out_shape=(shape, shape),
        in_specs=[pl.BlockSpec(memory_space=pl.ANY)] * 2,
        out_specs=(hbm, hbm),
        scratch_shapes=[pltpu.SemaphoreType.DMA((2,))],
        compiler_params=pltpu.CompilerParams(vmem_limit_bytes=1048576),
        name="store",
    )(final_position, final_speed)
    return tuple(jnp.transpose(x, (1, 0, 2)).reshape(3, node_count) for x in (final_position, final_speed))


def solution(mesh):
    in_specs = (
        P(None, ("parts", "wall")),
        P(None, ("parts", "wall")),
        P(("parts", "wall"), None, None),
        P(("parts", "wall"), None, None),
        P(("parts", "wall"), None),
        P(("parts", "wall"), None),
        P(("parts", "wall"), None, None),
        P(("parts", "wall")),
        P(),
    )
    out_specs = (P(None, ("parts", "wall")), P(None, ("parts", "wall")))
    return jax.shard_map(shards, mesh=mesh, in_specs=in_specs, out_specs=out_specs, check_vma=False)
```

time: 38.1 us -> 35.7 us (0.937)
  Pallas kernels: 37.3 us -> 34.7 us
    pallas_call x1, Pallas kernels: 36.5 us -> 33.9 us  [shards(): pl.pallas_call(functools.partial(force_kernel, blocks, width, nnz, peers)...]
where the time goes in v2:
time: 35.7 us; the launch traced here: 35.5 us
  Pallas kernels  34.7 us (97%)
  between operations  0.8 us (2%)
    pallas_call x1, Pallas kernels, shards(): pl.pallas_call(functools.partial(force_kernel, blocks, width, nnz, peers)...  33.9 us
    pallas_call x1, Pallas kernels, shards(): pl.pallas_call(store_kernel, out_shape=(shape, shape), in_specs=[pl.Block...  0.76 us

profile of v2, /device:TPU:5, one launch (start us, length us, event | category | flops | bytes accessed | tf_op | source)
XLA Modules:
  0.0 35.5 jit_solution(13648831654175211796)
XLA Ops:
  0.6 33.9 %forces.1 = (f32[128,3,128]{2,1,0:T(4,128)S(1)}, f32[128,3,128]{2,1,0:T(4,128)S(1)}) custom-call(s32[1,16,64]{2,1,0:T(8,128)} %send_hbm.1, s32[1,16,64]{2,1,0:T(8,128)} %arrive_hbm.1, s32[1,16]{1,0:T(1,128)} %count_hbm.1, s32[27,128]{1,0:T(8,128)} %bitcast.19, s32[27,128,128]{2,1,0:T(8,128)} %bitcast.15, f32[128,128]{1,0:T(8,128)} %bitcast.18, ...), custom_call_target="tpu_custom_call" | custom-call | tf_op jit(solution)/shard_map/forces/pallas_call | solution.py:524
  34.6 0.8 %store.1 = (f32[128,3,128]{2,1,0:T(4,128)}, f32[128,3,128]{2,1,0:T(4,128)}) custom-call(f32[128,3,128]{2,1,0:T(4,128)S(1)} %get-tuple-element.6.pos_in, f32[128,3,128]{2,1,0:T(4,128)S(1)} %get-tuple-element.7.vel_in), custom_call_target="tpu_custom_call" | custom-call | tf_op jit(solution)/shard_map/store/pallas_call | solution.py:584

commit v3 on v2

--- a/solution.py
+++ b/solution.py
@@ -44,8 +44,10 @@
     vel_raw,
     pos_in,
     vel_in,
-    out_buf,
-    in_buf,
+    out_pos,
+    in_pos,
+    out_vel,
+    in_vel,
     index_ref,
     node_ref,
     block_ref,
@@ -84,27 +86,27 @@
     capacity = send_ref.shape[1]
     shift = width.bit_length() - 1
     batch = math.gcd(PEER_BATCH, peers)
+    batches = peers // batch
     lane_count = batch * capacity
 
-    pairs = [(send_hbm.at[0], send_ref)]
-    pairs += [(pos_hbm, pos_raw), (vel_hbm, vel_raw)]
+    barrier = pltpu.get_barrier_semaphore()
+
+    def greet(step, carry):
+        pl.semaphore_signal(
+            barrier, inc=1, device_id={"wall": lax.rem(me + step, count)}, device_id_type=MESH
+        )
+        return carry
+
+    lax.fori_loop(1, peers, greet, 0)
+
+    pairs = [(send_hbm.at[0], send_ref), (pos_hbm, pos_raw)]
     early = len(pairs)
-    pairs += [(arrive_hbm.at[0], arrive_ref), (count_hbm, count_ref)]
+    pairs += [(vel_hbm, vel_raw), (arrive_hbm.at[0], arrive_ref), (count_hbm, count_ref)]
     listed = len(pairs)
     pairs += [(hor_hbm, hor_ref), (weight_hbm, weight_ref), (bonds_hbm, raw_ref), (mod_hbm, mod_ref)]
     fetches = [pltpu.make_async_copy(pair[0], pair[1], fetch_sem.at[i]) for i, pair in enumerate(pairs)]
     for fetch in fetches:
         fetch.start()
-
-    barrier = pltpu.get_barrier_semaphore()
-
-    def greet(step, carry):
-        pl.semaphore_signal(
-            barrier, inc=1, device_id={"wall": lax.rem(me + step, count)}, device_id_type=MESH
-        )
-        return carry
-
-    lax.fori_loop(1, peers, greet, 0)
 
     def split(value):
         high = value.astype(BF16)
@@ -171,21 +173,22 @@
             device_id_type=MESH,
         )
 
-    out_buf[...] = jnp.zeros(out_buf.shape, F32)
-    for fetch in fetches[:early]:
-        fetch.wait()
-    for row in range(3):
-        pos_in[row] = pos_raw[:, row, :]
-        vel_in[row] = vel_raw[:, row, :]
-    state = [pos_in, pos_in, pos_in, vel_in, vel_in, vel_in]
-
-    def gather_batch(step, carry):
+    def each_batch(body):
+        def step(index, carry):
+            body(index)
+            return carry
+
+        if batches == 1:
+            body(0)
+        else:
+            lax.fori_loop(0, batches, step, 0)
+
+    def pick(step, source):
         rows = send_ref[pl.ds(step * batch, batch), :]
         index = jnp.concatenate([rows[i : i + 1, :] for i in range(batch)], axis=1)
-        placed_rows = []
-        speed_rows = []
+        picked_rows = []
         tile = 256 if lane_count % 256 == 0 else lane_count
-        splits = [jnp.concatenate(split(state[row][row % 3]), axis=1) for row in range(6)]
+        splits = [jnp.concatenate(split(source[row]), axis=1) for row in range(3)]
         for start in range(0, lane_count, tile):
             part = index[:, start : start + tile]
             of_node = lax.broadcasted_iota(jnp.int32, (width, tile), 0) == (part & (width - 1))
@@ -193,53 +196,61 @@
             column = jnp.where(of_node, 1.0, 0.0).astype(BF16)
             column = jnp.concatenate([column, column], axis=0)
             values = []
-            for row in range(6):
+            for row in range(3):
                 found = jnp.dot(splits[row], column, preferred_element_type=F32)
                 values.append(jnp.sum(jnp.where(of_block, found, 0.0), axis=0, keepdims=True))
-            placed_rows.append(jnp.concatenate(values[:3] + values[:3], axis=0))
-            speed_rows.append(jnp.concatenate(values[3:], axis=0))
-        placed = jnp.concatenate(placed_rows, axis=1)
-        speeds = jnp.concatenate(speed_rows, axis=1)
+            picked_rows.append(values)
+        return [jnp.concatenate([values[row] for values in picked_rows], axis=1) for row in range(3)]
+
+    def gather_places(step):
+        values = pick(step, pos_in)
+        placed = jnp.concatenate(values + values, axis=0)
         for i in range(batch):
             peer = step * batch + i
             mine = slice(i * capacity, (i + 1) * capacity)
-            out_buf[peer + 1, 0:3, 0:capacity] = placed[0:3, mine]
-            out_buf[peer + 1, 0:3, capacity : 2 * capacity] = speeds[:, mine]
-            out_buf[peer + 2, 3:6, 0:capacity] = placed[3:6, mine]
-            out_buf[peer, 3:6, capacity : 2 * capacity] = placed[3:6, mine]
+            out_pos[peer + 1, 0:3, 0:capacity] = placed[0:3, mine]
+            out_pos[peer + 2, 0:3, capacity : 2 * capacity] = placed[0:3, mine]
+            out_pos[peer, 3:6, 0:capacity] = placed[3:6, mine]
+
+    def gather_speeds(step):
+        speeds = jnp.concatenate(pick(step, vel_in), axis=0)
+        for i in range(batch):
+            out_vel[step * batch + i, 0:3, 0:capacity] = speeds[:, i * capacity : (i + 1) * capacity]
+
+    def pos_copy(peer, there, many=1):
+        return pltpu.make_async_remote_copy(
+            src_ref=out_pos.at[pl.ds(peer, many), pl.ds(0, 6), :],
+            dst_ref=in_pos.at[pl.ds(there, many), pl.ds(0, 6), :],
+            send_sem=node_send_sem.at[0],
+            recv_sem=node_recv_sem.at[0],
+            device_id={"wall": neighbour(1)} if many > 1 else {"wall": peer - 1},
+            device_id_type=MESH,
+        )
+
+    def vel_copy(peer, there, many=1):
+        return pltpu.make_async_remote_copy(
+            src_ref=out_vel.at[pl.ds(peer, many), pl.ds(0, 3), :],
+            dst_ref=in_vel.at[pl.ds(there, many), pl.ds(0, 3), :],
+            send_sem=node_send_sem.at[1],
+            recv_sem=node_recv_sem.at[1],
+            device_id={"wall": neighbour(1)} if many > 1 else {"wall": peer},
+            device_id_type=MESH,
+        )
+
+    out_pos[...] = jnp.zeros(out_pos.shape, F32)
+    for fetch in fetches[:early]:
+        fetch.wait()
+    for row in range(3):
+        pos_in[row] = pos_raw[:, row, :]
+    each_batch(gather_places)
+    in_pos[me, 0:6, :] = out_pos[me + 1, 0:6, :]
+    pl.semaphore_wait(barrier, peers - 1)
+
+    def start_places(step, carry):
+        pos_copy(lax.rem(me + step, count) + 1, me).start()
         return carry
 
-    lax.fori_loop(0, peers // batch, gather_batch, 0)
-    in_buf[me, 0:6, :] = out_buf[me + 1, 0:6, :]
-    pl.semaphore_wait(barrier, peers - 1)
-
-    def node_copy(step):
-        peer = lax.rem(me + step, count)
-        return pltpu.make_async_remote_copy(
-            src_ref=out_buf.at[peer + 1, pl.ds(0, 6), :],
-            dst_ref=in_buf.at[me, pl.ds(0, 6), :],
-            send_sem=node_send_sem.at[peer],
-            recv_sem=node_recv_sem.at[me],
-            device_id={"wall": peer},
-            device_id_type=MESH,
-        )
-
-    def node_arrival(step):
-        peer = lax.rem(me + step, count)
-        return pltpu.make_async_remote_copy(
-            src_ref=out_buf.at[peer + 1, pl.ds(0, 6), :],
-            dst_ref=in_buf.at[peer, pl.ds(0, 6), :],
-            send_sem=node_send_sem.at[peer],
-            recv_sem=node_recv_sem.at[peer],
-            device_id={"wall": peer},
-            device_id_type=MESH,
-        )
-
-    def start_nodes(step, carry):
-        node_copy(step).start()
-        return carry
-
-    lax.fori_loop(1, peers, start_nodes, 0)
+    lax.fori_loop(1, peers, start_places, 0)
 
     for half in (0, 1):
         for row in range(3):
@@ -248,8 +259,11 @@
 
     for fetch in fetches[early:listed]:
         fetch.wait()
-
-    def index_batch(step, carry):
+    out_vel[...] = jnp.zeros(out_vel.shape, F32)
+    for row in range(3):
+        vel_in[row] = vel_raw[:, row, :]
+
+    def index_batch(step):
         rows = arrive_ref[pl.ds(step * batch, batch), :]
         slot_ids = lax.broadcasted_iota(jnp.int32, (1, capacity), 1)
         index_ref[1, step] = jnp.concatenate(
@@ -259,9 +273,8 @@
             ],
             axis=1,
         )
-        return carry
-
-    lax.fori_loop(0, peers // batch, index_batch, 0)
+
+    each_batch(index_batch)
     for half in (0, 1):
 
         @pl.when(exists(half))
@@ -273,6 +286,15 @@
             index_ref[2 * half] = jnp.full(index_ref.shape[1:], nodes, jnp.int32)
             for slot in range(slots):
                 ext_ref[slot, pl.ds(3 * LAYER * half, LAYER), :] = jnp.zeros((LAYER, 4 * width), BF16)
+
+    each_batch(gather_speeds)
+    in_vel[me, 0:3, :] = out_vel[me, 0:3, :]
+
+    def start_speeds(step, carry):
+        vel_copy(lax.rem(me + step, count), me).start()
+        return carry
+
+    lax.fori_loop(1, peers, start_speeds, 0)
 
     lanes = lax.broadcasted_iota(jnp.int32, (LAYER, reach), 1)
     fetches[listed].wait()
@@ -303,7 +325,20 @@
         def _():
             index_copy(1 - half).wait_recv()
 
-    def mark_batch(step, carry):
+    def gain(ref, value):
+        ref[...] = value if batches == 1 else ref[...] + value
+
+    def clear(refs):
+        if batches > 1:
+            for ref in refs:
+                ref[...] = jnp.zeros(ref.shape, F32)
+
+    def land(marks, which, step):
+        return lax.dot_general(
+            marks, node_ref[which, step], (((1,), (1,)), ((), ())), preferred_element_type=F32
+        )
+
+    def mark_batch(step):
         for which in range(3):
             index = index_ref[which, step]
             of_node = lax.broadcasted_iota(jnp.int32, (width, lane_count), 0) == (index & (width - 1))
@@ -312,72 +347,82 @@
             first = LAYER if which == 0 else 0
             of_block = lax.broadcasted_iota(jnp.int32, (depth, lane_count), 0) + first == (index >> shift)
             marks = jnp.where(of_block, 1.0, 0.0).astype(BF16)
-            start = (blocks + LAYER, 0, blocks)[which]
-            block_ref[step, pl.ds(start, depth), :] = marks
-            hit_ref[pl.ds(start, depth), :] = hit_ref[pl.ds(start, depth), :] + lax.dot_general(
-                marks, node_ref[which, step], (((1,), (1,)), ((), ())), preferred_element_type=F32
-            )
-        return carry
-
-    hit_ref[...] = jnp.zeros(hit_ref.shape, F32)
-    lax.fori_loop(0, peers // batch, mark_batch, 0)
-
-    landed_ref[...] = jnp.zeros(landed_ref.shape, F32)
-    ghost_landed_ref[...] = jnp.zeros(ghost_landed_ref.shape, F32)
+            rows = pl.ds((blocks + LAYER, 0, blocks)[which], depth)
+            block_ref[step, rows, :] = marks
+            gain(hit_ref.at[rows], land(marks, which, step))
+
+    clear([hit_ref])
+    each_batch(mark_batch)
+    clear([landed_ref, ghost_landed_ref])
 
     for half in (0, 1):
         wait_halo(0, half, 0, lanes_of(0, 3))
         wait_sent(0, half, 0, lanes_of(0, 3))
 
-    def finish_nodes(step, carry):
-        node_arrival(step).wait()
-        return carry
-
-    lax.fori_loop(1, peers, finish_nodes, 0)
-
-    def scatter_batch(step, carry):
-        bundles = [in_buf[step * batch + i, 0:6, :] for i in range(batch)]
+    def places(step):
+        bundles = [in_pos[step * batch + i, 0:6, :] for i in range(batch)]
         first = jnp.concatenate([bundle[:, 0:capacity] for bundle in bundles], axis=1)
-        second = jnp.concatenate([bundle[:, capacity : 2 * capacity] for bundle in bundles], axis=1)
+        left = jnp.concatenate([bundle[0:3, capacity : 2 * capacity] for bundle in bundles], axis=1)
+        return first[0:3], left, first[3:6]
+
+    def ghost_rows(half):
+        return pl.ds(pl.multiple_of(blocks + LAYER - half * LAYER, LAYER), LAYER)
+
+    def land_ghost(step, half, values):
+        rounded = values.astype(BF16)
+        for row in range(3):
+            ghost_spread_ref[pl.ds(row * LAYER, LAYER), :] = (
+                block_ref[step, ghost_rows(half), :] * rounded[row : row + 1, :]
+            )
+        gain(ghost_landed_ref.at[half], land(ghost_spread_ref[...], 2 * half, step))
+
+    def keep_ghost(half):
+        hit = hit_ref[ghost_rows(half), :] > 0.5
+        rows = pl.ds(pl.multiple_of(3 * LAYER * half, LAYER), LAYER)
+        for row in range(3):
+            landed = ghost_landed_ref[half, pl.ds(row * LAYER, LAYER), :]
+            held_now = ext_ref[0, rows, lanes_of(row, 1)].astype(F32)
+            ext_ref[0, rows, lanes_of(row, 1)] = jnp.where(hit, landed, held_now).astype(BF16)
+
+    def spread(step, section, rounded):
         marks = block_ref[step, pl.ds(0, blocks), :]
-        for k, values in enumerate((first, second)):
-            parts = split(values)
-            for row in range(3):
-                for low in range(2):
-                    spread_ref[pl.ds((6 * k + 2 * row + low) * blocks, blocks), :] = (
-                        marks * parts[low][row : row + 1, :]
-                    )
-                side = pl.ds(blocks + LAYER - k * LAYER, LAYER)
-                ghost_spread_ref[k, pl.ds(row * LAYER, LAYER), :] = (
-                    block_ref[step, side, :] * parts[0][3 + row : 4 + row, :]
-                )
-            ghost_landed_ref[k] = ghost_landed_ref[k] + lax.dot_general(
-                ghost_spread_ref[k], node_ref[2 * k, step], (((1,), (1,)), ((), ())), preferred_element_type=F32
-            )
-        landed_ref[...] = landed_ref[...] + lax.dot_general(
-            spread_ref[...], node_ref[1, step], (((1,), (1,)), ((), ())), preferred_element_type=F32
-        )
-        return carry
-
-    lax.fori_loop(0, peers // batch, scatter_batch, 0)
-
-    for k in (0, 1):
-        hit = hit_ref[pl.ds(blocks + LAYER - k * LAYER, LAYER), :] > 0.5
-        for row in range(3):
-            where = (0, pl.ds(3 * LAYER * k, LAYER), lanes_of(row, 1))
-            landed = ghost_landed_ref[k, pl.ds(row * LAYER, LAYER), :]
-            ext_ref[where] = jnp.where(hit, landed, ext_ref[where].astype(F32)).astype(BF16)
+        for row in range(3):
+            spread_ref[pl.ds((3 * section + row) * blocks, blocks), :] = marks * rounded[row : row + 1, :]
+
+    def land_section(step, section, pieces):
+        for first, rows in pieces:
+            rows_of = pl.ds((3 * section + first) * blocks, rows * blocks)
+            gain(landed_ref.at[rows_of], land(spread_ref[rows_of, :], 1, step))
+
+    def land_first(step):
+        mine, left, right = places(step)
+        spread(step, 0, mine.astype(BF16))
+        land_ghost(step, slow, jnp.where(slow == 0, left, right))
+        land_section(step, 0, ((0, 2), (2, 1)))
+
+    def land_fast(step):
+        _, left, right = places(step)
+        land_ghost(step, fast, jnp.where(fast == 0, left, right))
+
+    def land_rest(step):
+        mine, _, _ = places(step)
+        speeds = jnp.concatenate(
+            [in_vel[step * batch + i, 0:3, :][:, 0:capacity] for i in range(batch)], axis=1
+        )
+        spread(step, 1, split(mine)[1])
+        for part, rounded in enumerate(split(speeds)):
+            spread(step, 2 + part, rounded)
+        for section in (1, 2, 3):
+            land_section(step, section, ((0, 3),))
+
+    pos_copy(0, 0, peers - 1).wait_recv()
+    each_batch(land_first)
+    keep_ghost(slow)
     for half in (0, 1):
         hit = hit_ref[own(half), :] > 0.5
-        for row in range(6):
-            high = landed_ref[pl.ds(2 * row * blocks + half * LAYER, LAYER), :]
-            low = landed_ref[pl.ds((2 * row + 1) * blocks + half * LAYER, LAYER), :]
-            value = jnp.where(hit, high + low, state[row][row % 3, own(half), :])
-            if row < 3:
-                pos_ref[row, own(half), :] = value
-                put(0, half, row, value.astype(BF16))
-            else:
-                vel_ref[row - 3, own(half), :] = value
+        for row in range(3):
+            landed = landed_ref[pl.ds(row * blocks + half * LAYER, LAYER), :]
+            put(0, half, row, jnp.where(hit, landed, get(0, half, row)).astype(BF16))
 
     group = 9 if nnz % 9 == 0 else nnz
 
@@ -459,7 +504,20 @@
                 send(near + 2, half, part, lanes_of(*near_parts(apart)[part]))
 
     stretching(0, slow, True, False)
+    each_batch(land_fast)
+    keep_ghost(fast)
     stretching(0, fast, False, False)
+
+    vel_copy(0, 0, peers - 1).wait_recv()
+    each_batch(land_rest)
+    for half in (0, 1):
+        hit = hit_ref[own(half), :] > 0.5
+        for row in range(3):
+            parts = [
+                landed_ref[pl.ds((3 * section + row) * blocks + half * LAYER, LAYER), :] for section in range(4)
+            ]
+            pos_ref[row, own(half), :] = jnp.where(hit, parts[0] + parts[1], pos_in[row, own(half), :])
+            vel_ref[row, own(half), :] = jnp.where(hit, parts[2] + parts[3], vel_in[row, own(half), :])
 
     def substep(t, carry):
         pairing(t, fast, False, False)
@@ -475,6 +533,8 @@
     pairing(SUBSTEPS, fast, False, True)
     pairing(SUBSTEPS, slow, True, True)
 
+    pos_copy(0, 0, peers - 1).wait_send()
+    vel_copy(0, 0, peers - 1).wait_send()
     for half in (0, 1):
 
         @pl.when(exists(half))
@@ -539,13 +599,15 @@
             pltpu.VMEM((3, blocks, width), F32),
             pltpu.VMEM((peers + 2, 8, bundle_width), F32),
             pltpu.VMEM((peers, 8, bundle_width), F32),
+            pltpu.VMEM((peers, 8, bundle_width), F32),
+            pltpu.VMEM((peers, 8, bundle_width), F32),
             pltpu.VMEM((3, batches, 1, lane_count), jnp.int32),
             pltpu.VMEM((3, batches, width, lane_count), BF16),
             pltpu.VMEM((batches, blocks + 2 * LAYER, lane_count), BF16),
             pltpu.VMEM((blocks + 2 * LAYER, width), F32),
             pltpu.VMEM((12 * blocks, lane_count), BF16),
             pltpu.VMEM((12 * blocks, width), F32),
-            pltpu.VMEM((2, 3 * LAYER, lane_count), BF16),
+            pltpu.VMEM((3 * LAYER, lane_count), BF16),
             pltpu.VMEM((2, 3 * LAYER, width), F32),
             pltpu.VMEM((nnz, blocks, width), jnp.int32),
             pltpu.VMEM((nnz, blocks, width), F32),
@@ -562,8 +624,8 @@
             pltpu.SemaphoreType.DMA((slots, 2, 2)),
             pltpu.SemaphoreType.DMA((2,)),
             pltpu.SemaphoreType.DMA((2,)),
-            pltpu.SemaphoreType.DMA((peers,)),
-            pltpu.SemaphoreType.DMA((peers,)),
+            pltpu.SemaphoreType.DMA((2,)),
+            pltpu.SemaphoreType.DMA((2,)),
             pltpu.SemaphoreType.DMA((9,)),
         ],
         compiler_params=pltpu.CompilerParams(

time: 35.7 us -> 34.4 us (0.964)
  Pallas kernels: 34.7 us -> 33.3 us
    pallas_call x1, Pallas kernels: 33.9 us -> 32.6 us  [shards(): pl.pallas_call(functools.partial(force_kernel, blocks, width, nnz, peers)...]
where the time goes in v3:
time: 34.4 us; the launch traced here: 34.1 us
  Pallas kernels  33.3 us (97%)
  between operations  0.8 us (2%)
    pallas_call x1, Pallas kernels, shards(): pl.pallas_call(functools.partial(force_kernel, blocks, width, nnz, peers)...  32.6 us
    pallas_call x1, Pallas kernels, shards(): pl.pallas_call(store_kernel, out_shape=(shape, shape), in_specs=[pl.Block...  0.76 us

profile of v3, /device:TPU:5, one launch (start us, length us, event | category | flops | bytes accessed | tf_op | source)
XLA Modules:
  0.0 34.1 jit_solution(9024672597725844875)
XLA Ops:
  0.6 32.6 %forces.1 = (f32[128,3,128]{2,1,0:T(4,128)S(1)}, f32[128,3,128]{2,1,0:T(4,128)S(1)}) custom-call(s32[1,16,64]{2,1,0:T(8,128)} %send_hbm.1, s32[1,16,64]{2,1,0:T(8,128)} %arrive_hbm.1, s32[1,16]{1,0:T(1,128)} %count_hbm.1, s32[27,128]{1,0:T(8,128)} %bitcast.19, s32[27,128,128]{2,1,0:T(8,128)} %bitcast.15, f32[128,128]{1,0:T(8,128)} %bitcast.18, ...), custom_call_target="tpu_custom_call" | custom-call | tf_op jit(solution)/shard_map/forces/pallas_call | solution.py:584
  33.2 0.8 %store.1 = (f32[128,3,128]{2,1,0:T(4,128)}, f32[128,3,128]{2,1,0:T(4,128)}) custom-call(f32[128,3,128]{2,1,0:T(4,128)S(1)} %get-tuple-element.6.pos_in, f32[128,3,128]{2,1,0:T(4,128)S(1)} %get-tuple-element.7.vel_in), custom_call_target="tpu_custom_call" | custom-call | tf_op jit(solution)/shard_map/store/pallas_call | solution.py:646

commit v4 on v3

--- a/solution.py
+++ b/solution.py
@@ -48,6 +48,8 @@
     in_pos,
     out_vel,
     in_vel,
+    leave_node_ref,
+    leave_block_ref,
     index_ref,
     node_ref,
     block_ref,
@@ -99,14 +101,23 @@
 
     lax.fori_loop(1, peers, greet, 0)
 
-    pairs = [(send_hbm.at[0], send_ref), (pos_hbm, pos_raw)]
-    early = len(pairs)
-    pairs += [(vel_hbm, vel_raw), (arrive_hbm.at[0], arrive_ref), (count_hbm, count_ref)]
-    listed = len(pairs)
-    pairs += [(hor_hbm, hor_ref), (weight_hbm, weight_ref), (bonds_hbm, raw_ref), (mod_hbm, mod_ref)]
-    fetches = [pltpu.make_async_copy(pair[0], pair[1], fetch_sem.at[i]) for i, pair in enumerate(pairs)]
-    for fetch in fetches:
-        fetch.start()
+    pairs = {
+        "send": (send_hbm.at[0], send_ref),
+        "pos": (pos_hbm, pos_raw),
+        "arrive": (arrive_hbm.at[0], arrive_ref),
+        "count": (count_hbm, count_ref),
+        "hor": (hor_hbm, hor_ref),
+        "weight": (weight_hbm, weight_ref),
+        "bonds": (bonds_hbm, raw_ref),
+        "mod": (mod_hbm, mod_ref),
+        "vel": (vel_hbm, vel_raw),
+    }
+    fetches = {
+        name: pltpu.make_async_copy(pair[0], pair[1], fetch_sem.at[i])
+        for i, (name, pair) in enumerate(pairs.items())
+    }
+    for name in ("send", "pos", "arrive", "count", "hor"):
+        fetches[name].start()
 
     def split(value):
         high = value.astype(BF16)
@@ -183,22 +194,35 @@
         else:
             lax.fori_loop(0, batches, step, 0)
 
-    def pick(step, source):
+    def apart(body):
+        def once(step, carry):
+            body()
+            return carry
+
+        lax.fori_loop(0, 1 + lax.div(me, count), once, 0)
+
+    def mark_leaving(step):
         rows = send_ref[pl.ds(step * batch, batch), :]
         index = jnp.concatenate([rows[i : i + 1, :] for i in range(batch)], axis=1)
-        picked_rows = []
+        of_node = lax.broadcasted_iota(jnp.int32, (width, lane_count), 0) == (index & (width - 1))
+        of_block = lax.broadcasted_iota(jnp.int32, (blocks, lane_count), 0) == (index >> shift)
+        column = jnp.where(of_node, 1.0, 0.0).astype(BF16)
+        leave_node_ref[step, 0:width, :] = column
+        leave_node_ref[step, width : 2 * width, :] = column
+        leave_block_ref[step] = jnp.where(of_block, 1.0, 0.0)
+
+    def pick(step, source):
         tile = 256 if lane_count % 256 == 0 else lane_count
         splits = [jnp.concatenate(split(source[row]), axis=1) for row in range(3)]
+        picked_rows = []
         for start in range(0, lane_count, tile):
-            part = index[:, start : start + tile]
-            of_node = lax.broadcasted_iota(jnp.int32, (width, tile), 0) == (part & (width - 1))
-            of_block = lax.broadcasted_iota(jnp.int32, (blocks, tile), 0) == (part >> shift)
-            column = jnp.where(of_node, 1.0, 0.0).astype(BF16)
-            column = jnp.concatenate([column, column], axis=0)
+            of_block = leave_block_ref[step, :, start : start + tile]
             values = []
             for row in range(3):
-                found = jnp.dot(splits[row], column, preferred_element_type=F32)
-                values.append(jnp.sum(jnp.where(of_block, found, 0.0), axis=0, keepdims=True))
+                found = jnp.dot(
+                    splits[row], leave_node_ref[step, :, start : start + tile], preferred_element_type=F32
+                )
+                values.append(jnp.sum(of_block * found, axis=0, keepdims=True))
             picked_rows.append(values)
         return [jnp.concatenate([values[row] for values in picked_rows], axis=1) for row in range(3)]
 
@@ -238,31 +262,6 @@
         )
 
     out_pos[...] = jnp.zeros(out_pos.shape, F32)
-    for fetch in fetches[:early]:
-        fetch.wait()
-    for row in range(3):
-        pos_in[row] = pos_raw[:, row, :]
-    each_batch(gather_places)
-    in_pos[me, 0:6, :] = out_pos[me + 1, 0:6, :]
-    pl.semaphore_wait(barrier, peers - 1)
-
-    def start_places(step, carry):
-        pos_copy(lax.rem(me + step, count) + 1, me).start()
-        return carry
-
-    lax.fori_loop(1, peers, start_places, 0)
-
-    for half in (0, 1):
-        for row in range(3):
-            put(0, half, row, pos_in[row, own(half), :].astype(BF16))
-        send(0, half, 0, lanes_of(0, 3))
-
-    for fetch in fetches[early:listed]:
-        fetch.wait()
-    out_vel[...] = jnp.zeros(out_vel.shape, F32)
-    for row in range(3):
-        vel_in[row] = vel_raw[:, row, :]
-
     def index_batch(step):
         rows = arrive_ref[pl.ds(step * batch, batch), :]
         slot_ids = lax.broadcasted_iota(jnp.int32, (1, capacity), 1)
@@ -274,7 +273,26 @@
             axis=1,
         )
 
+    fetches["send"].wait()
+    each_batch(mark_leaving)
+    for name in ("arrive", "count"):
+        fetches[name].wait()
     each_batch(index_batch)
+    fetches["pos"].wait()
+    for name in ("weight", "bonds", "mod", "vel"):
+        fetches[name].start()
+    for row in range(3):
+        pos_in[row] = pos_raw[:, row, :]
+    each_batch(gather_places)
+    in_pos[me, 0:6, :] = out_pos[me + 1, 0:6, :]
+    pl.semaphore_wait(barrier, peers - 1)
+
+    def start_places(step, carry):
+        pos_copy(lax.rem(me + step, count) + 1, me).start()
+        return carry
+
+    lax.fori_loop(1, peers, start_places, 0)
+
     for half in (0, 1):
 
         @pl.when(exists(half))
@@ -287,17 +305,13 @@
             for slot in range(slots):
                 ext_ref[slot, pl.ds(3 * LAYER * half, LAYER), :] = jnp.zeros((LAYER, 4 * width), BF16)
 
-    each_batch(gather_speeds)
-    in_vel[me, 0:3, :] = out_vel[me, 0:3, :]
-
-    def start_speeds(step, carry):
-        vel_copy(lax.rem(me + step, count), me).start()
-        return carry
-
-    lax.fori_loop(1, peers, start_speeds, 0)
+    for half in (0, 1):
+        for row in range(3):
+            put(0, half, row, pos_in[row, own(half), :].astype(BF16))
+        send(0, half, 0, lanes_of(0, 3))
 
     lanes = lax.broadcasted_iota(jnp.int32, (LAYER, reach), 1)
-    fetches[listed].wait()
+    fetches["hor"].wait()
     padding = jnp.zeros((-nnz % 8, blocks), jnp.int32)
     horizon = jnp.transpose(jnp.concatenate([hor_ref[...], padding], axis=0))
     for half in range(2):
@@ -306,8 +320,22 @@
             hit = local[:, j : j + 1] == lanes
             onehot_ref[half, pl.ds(j * LAYER, LAYER), :] = jnp.where(hit, 1.0, 0.0).astype(BF16)
 
-    for fetch in fetches[listed + 1 :]:
-        fetch.wait()
+    fetches["vel"].wait()
+    out_vel[...] = jnp.zeros(out_vel.shape, F32)
+    for row in range(3):
+        vel_in[row] = vel_raw[:, row, :]
+
+    each_batch(gather_speeds)
+    in_vel[me, 0:3, :] = out_vel[me, 0:3, :]
+
+    def start_speeds(step, carry):
+        vel_copy(lax.rem(me + step, count), me).start()
+        return carry
+
+    lax.fori_loop(1, peers, start_speeds, 0)
+
+    for name in ("weight", "bonds", "mod"):
+        fetches[name].wait()
     stiff = jnp.zeros((blocks, width), F32)
     ones = jnp.ones((16, width), BF16)
     for j in range(nnz):
@@ -416,13 +444,16 @@
             land_section(step, section, ((0, 3),))
 
     pos_copy(0, 0, peers - 1).wait_recv()
-    each_batch(land_first)
-    keep_ghost(slow)
-    for half in (0, 1):
-        hit = hit_ref[own(half), :] > 0.5
-        for row in range(3):
-            landed = landed_ref[pl.ds(row * blocks + half * LAYER, LAYER), :]
-            put(0, half, row, jnp.where(hit, landed, get(0, half, row)).astype(BF16))
+
+    @apart
+    def _():
+        each_batch(land_first)
+        keep_ghost(slow)
+        for half in (0, 1):
+            hit = hit_ref[own(half), :] > 0.5
+            for row in range(3):
+                landed = landed_ref[pl.ds(row * blocks + half * LAYER, LAYER), :]
+                put(0, half, row, jnp.where(hit, landed, get(0, half, row)).astype(BF16))
 
     group = 9 if nnz % 9 == 0 else nnz
 
@@ -447,16 +478,16 @@
                 sums[row] = sums[row] + product[row * LAYER : (row + 1) * LAYER] * mask
         return sums
 
-    def near_parts(apart):
-        return ((0, 1), (1, 2)) if apart else ((0, 3),)
-
-    def far_parts(apart):
-        return ((0, 2), (2, 2)) if apart else ((0, 4),)
-
-    def stretching(t, half, apart, waits):
+    def near_parts(parted):
+        return ((0, 1), (1, 2)) if parted else ((0, 3),)
+
+    def far_parts(parted):
+        return ((0, 2), (2, 2)) if parted else ((0, 4),)
+
+    def stretching(t, half, parted, waits):
         near, far = 2 * t, 2 * t + 1
         summed = []
-        for part, (first, rows) in enumerate(near_parts(apart)):
+        for part, (first, rows) in enumerate(near_parts(parted and waits)):
             if waits:
                 wait_halo(near, half, part, lanes_of(first, rows))
             summed += contract(near, first, rows, half)
@@ -471,19 +502,19 @@
         put(far, half, 0, soft_low)
         for row in range(3):
             put(far, half, 1 + row, (soft_wide * rounded[row]).astype(BF16))
-        for part, (first, rows) in enumerate(far_parts(apart)):
+        for part, (first, rows) in enumerate(far_parts(parted)):
             send(far, half, part, lanes_of(first, rows))
         for row in range(3):
             stretch_ref[row, own(half), :] = stretch[row]
         soften_ref[own(half), :] = soften
 
-    def pairing(t, half, apart, last):
+    def pairing(t, half, parted, last):
         near, far = 2 * t, 2 * t + 1
         scaling = mod_ref[own(half), :]
         soften = soften_ref[own(half), :]
         kick = 0.5 * TIME_STEP if last else jnp.where(t == 0, 0.5 * TIME_STEP, TIME_STEP)
         paired = []
-        for part, (first, rows) in enumerate(far_parts(apart)):
+        for part, (first, rows) in enumerate(far_parts(parted)):
             wait_halo(far, half, part, lanes_of(first, rows))
             begin = max(len(paired) - 1, 0)
             paired += contract(far, first, rows, half)
@@ -501,11 +532,15 @@
                     pos_ref[row, own(half), :] = moved
                     put(near + 2, half, row, moved.astype(BF16))
             if not last:
-                send(near + 2, half, part, lanes_of(*near_parts(apart)[part]))
+                send(near + 2, half, part, lanes_of(*near_parts(parted)[part]))
 
     stretching(0, slow, True, False)
-    each_batch(land_fast)
-    keep_ghost(fast)
+
+    @apart
+    def _():
+        each_batch(land_fast)
+        keep_ghost(fast)
+
     stretching(0, fast, False, False)
 
     vel_copy(0, 0, peers - 1).wait_recv()
@@ -542,8 +577,8 @@
             index_copy(half).wait_send()
 
     for slot in range(1, slots):
-        for half, apart in ((fast, False), (slow, True)):
-            parts = far_parts(apart) if slot % 2 else near_parts(apart)
+        for half, parted in ((fast, False), (slow, True)):
+            parts = far_parts(parted) if slot % 2 else near_parts(parted)
             for part, (first, rows) in enumerate(parts):
                 wait_sent(slot, half, part, lanes_of(first, rows))
 
@@ -601,6 +636,8 @@
             pltpu.VMEM((peers, 8, bundle_width), F32),
             pltpu.VMEM((peers, 8, bundle_width), F32),
             pltpu.VMEM((peers, 8, bundle_width), F32),
+            pltpu.VMEM((batches, 2 * width, lane_count), BF16),
+            pltpu.VMEM((batches, blocks, lane_count), F32),
             pltpu.VMEM((3, batches, 1, lane_count), jnp.int32),
             pltpu.VMEM((3, batches, width, lane_count), BF16),
             pltpu.VMEM((batches, blocks + 2 * LAYER, lane_count), BF16),

time: 34.4 us -> 33.7 us (0.980)
  Pallas kernels: 33.3 us -> 32.7 us
    pallas_call x1, Pallas kernels: 32.6 us -> 32 us  [shards(): pl.pallas_call(functools.partial(force_kernel, blocks, width, nnz, peers)...]
where the time goes in v4:
time: 33.7 us; the launch traced here: 33.5 us
  Pallas kernels  32.7 us (97%)
  between operations  0.8 us (2%)
    pallas_call x1, Pallas kernels, shards(): pl.pallas_call(functools.partial(force_kernel, blocks, width, nnz, peers)...  32 us
    pallas_call x1, Pallas kernels, shards(): pl.pallas_call(store_kernel, out_shape=(shape, shape), in_specs=[pl.Block...  0.76 us

profile of v4, /device:TPU:5, one launch (start us, length us, event | category | flops | bytes accessed | tf_op | source)
XLA Modules:
  0.0 33.5 jit_solution(15223660119350947447)
XLA Ops:
  0.6 32.0 %forces.1 = (f32[128,3,128]{2,1,0:T(4,128)S(1)}, f32[128,3,128]{2,1,0:T(4,128)S(1)}) custom-call(s32[1,16,64]{2,1,0:T(8,128)} %send_hbm.1, s32[1,16,64]{2,1,0:T(8,128)} %arrive_hbm.1, s32[1,16]{1,0:T(1,128)} %count_hbm.1, s32[27,128]{1,0:T(8,128)} %bitcast.19, s32[27,128,128]{2,1,0:T(8,128)} %bitcast.15, f32[128,128]{1,0:T(8,128)} %bitcast.18, ...), custom_call_target="tpu_custom_call" | custom-call | tf_op jit(solution)/shard_map/forces/pallas_call | solution.py:619
  32.6 0.8 %store.1 = (f32[128,3,128]{2,1,0:T(4,128)}, f32[128,3,128]{2,1,0:T(4,128)}) custom-call(f32[128,3,128]{2,1,0:T(4,128)S(1)} %get-tuple-element.6.pos_in, f32[128,3,128]{2,1,0:T(4,128)S(1)} %get-tuple-element.7.vel_in), custom_call_target="tpu_custom_call" | custom-call | tf_op jit(solution)/shard_map/store/pallas_call | solution.py:683

commit v5 on v4

--- a/solution.py
+++ b/solution.py
@@ -361,23 +361,33 @@
             for ref in refs:
                 ref[...] = jnp.zeros(ref.shape, F32)
 
-    def land(marks, which, step):
+    def columns_of(which):
+        if isinstance(which, int):
+            return pl.ds((0, 2 * width, width)[which], 2 * width if which == 1 else width)
+        return pl.ds(pl.multiple_of(lax.div(which, 2) * width, width), width)
+
+    def land(marks, columns, step):
         return lax.dot_general(
-            marks, node_ref[which, step], (((1,), (1,)), ((), ())), preferred_element_type=F32
+            marks, node_ref[step, columns, :], (((1,), (1,)), ((), ())), preferred_element_type=F32
         )
 
     def mark_batch(step):
         for which in range(3):
             index = index_ref[which, step]
-            of_node = lax.broadcasted_iota(jnp.int32, (width, lane_count), 0) == (index & (width - 1))
-            node_ref[which, step] = jnp.where(of_node, 1.0, 0.0).astype(BF16)
-            depth = blocks if which == 1 else LAYER
+            inside = index & (width - 1)
+            block = index >> shift
+            if which == 1:
+                inside = inside + jnp.where(block >= LAYER, width, 0)
+                block = jnp.where(block < 2 * LAYER, block & (LAYER - 1), 2 * LAYER)
             first = LAYER if which == 0 else 0
-            of_block = lax.broadcasted_iota(jnp.int32, (depth, lane_count), 0) + first == (index >> shift)
+            columns = columns_of(which)
+            of_node = lax.broadcasted_iota(jnp.int32, (columns.size, lane_count), 0) == inside
+            node_ref[step, columns, :] = jnp.where(of_node, 1.0, 0.0).astype(BF16)
+            of_block = lax.broadcasted_iota(jnp.int32, (LAYER, lane_count), 0) + first == block
             marks = jnp.where(of_block, 1.0, 0.0).astype(BF16)
-            rows = pl.ds((blocks + LAYER, 0, blocks)[which], depth)
+            rows = pl.ds(which * LAYER, LAYER)
             block_ref[step, rows, :] = marks
-            gain(hit_ref.at[rows], land(marks, which, step))
+            gain(hit_ref.at[:, columns], land(marks, columns, step))
 
     clear([hit_ref])
     each_batch(mark_batch)
@@ -394,7 +404,7 @@
         return first[0:3], left, first[3:6]
 
     def ghost_rows(half):
-        return pl.ds(pl.multiple_of(blocks + LAYER - half * LAYER, LAYER), LAYER)
+        return pl.ds(pl.multiple_of(2 * half * LAYER, LAYER), LAYER)
 
     def land_ghost(step, half, values):
         rounded = values.astype(BF16)
@@ -402,10 +412,10 @@
             ghost_spread_ref[pl.ds(row * LAYER, LAYER), :] = (
                 block_ref[step, ghost_rows(half), :] * rounded[row : row + 1, :]
             )
-        gain(ghost_landed_ref.at[half], land(ghost_spread_ref[...], 2 * half, step))
+        gain(ghost_landed_ref.at[half], land(ghost_spread_ref[...], columns_of(2 * half), step))
 
     def keep_ghost(half):
-        hit = hit_ref[ghost_rows(half), :] > 0.5
+        hit = hit_ref[:, columns_of(2 * half)] > 0.5
         rows = pl.ds(pl.multiple_of(3 * LAYER * half, LAYER), LAYER)
         for row in range(3):
             landed = ghost_landed_ref[half, pl.ds(row * LAYER, LAYER), :]
@@ -413,20 +423,26 @@
             ext_ref[0, rows, lanes_of(row, 1)] = jnp.where(hit, landed, held_now).astype(BF16)
 
     def spread(step, section, rounded):
-        marks = block_ref[step, pl.ds(0, blocks), :]
+        marks = block_ref[step, pl.ds(LAYER, LAYER), :]
         for row in range(3):
-            spread_ref[pl.ds((3 * section + row) * blocks, blocks), :] = marks * rounded[row : row + 1, :]
+            spread_ref[pl.ds((3 * section + row) * LAYER, LAYER), :] = marks * rounded[row : row + 1, :]
 
     def land_section(step, section, pieces):
         for first, rows in pieces:
-            rows_of = pl.ds((3 * section + first) * blocks, rows * blocks)
-            gain(landed_ref.at[rows_of], land(spread_ref[rows_of, :], 1, step))
+            rows_of = pl.ds((3 * section + first) * LAYER, rows * LAYER)
+            gain(landed_ref.at[rows_of], land(spread_ref[rows_of, :], columns_of(1), step))
+
+    def own_columns(half):
+        return pl.ds(half * width, width)
+
+    def own_hit(half):
+        return hit_ref[:, pl.ds((2 + half) * width, width)] > 0.5
 
     def land_first(step):
         mine, left, right = places(step)
         spread(step, 0, mine.astype(BF16))
         land_ghost(step, slow, jnp.where(slow == 0, left, right))
-        land_section(step, 0, ((0, 2), (2, 1)))
+        land_section(step, 0, ((0, 3),))
 
     def land_fast(step):
         _, left, right = places(step)
@@ -450,9 +466,9 @@
         each_batch(land_first)
         keep_ghost(slow)
         for half in (0, 1):
-            hit = hit_ref[own(half), :] > 0.5
+            hit = own_hit(half)
             for row in range(3):
-                landed = landed_ref[pl.ds(row * blocks + half * LAYER, LAYER), :]
+                landed = landed_ref[pl.ds(row * LAYER, LAYER), own_columns(half)]
                 put(0, half, row, jnp.where(hit, landed, get(0, half, row)).astype(BF16))
 
     group = 9 if nnz % 9 == 0 else nnz
@@ -546,10 +562,10 @@
     vel_copy(0, 0, peers - 1).wait_recv()
     each_batch(land_rest)
     for half in (0, 1):
-        hit = hit_ref[own(half), :] > 0.5
+        hit = own_hit(half)
         for row in range(3):
             parts = [
-                landed_ref[pl.ds((3 * section + row) * blocks + half * LAYER, LAYER), :] for section in range(4)
+                landed_ref[pl.ds((3 * section + row) * LAYER, LAYER), own_columns(half)] for section in range(4)
             ]
             pos_ref[row, own(half), :] = jnp.where(hit, parts[0] + parts[1], pos_in[row, own(half), :])
             vel_ref[row, own(half), :] = jnp.where(hit, parts[2] + parts[3], vel_in[row, own(half), :])
@@ -639,11 +655,11 @@
             pltpu.VMEM((batches, 2 * width, lane_count), BF16),
             pltpu.VMEM((batches, blocks, lane_count), F32),
             pltpu.VMEM((3, batches, 1, lane_count), jnp.int32),
-            pltpu.VMEM((3, batches, width, lane_count), BF16),
-            pltpu.VMEM((batches, blocks + 2 * LAYER, lane_count), BF16),
-            pltpu.VMEM((blocks + 2 * LAYER, width), F32),
-            pltpu.VMEM((12 * blocks, lane_count), BF16),
-            pltpu.VMEM((12 * blocks, width), F32),
+            pltpu.VMEM((batches, 4 * width, lane_count), BF16),
+            pltpu.VMEM((batches, 3 * LAYER, lane_count), BF16),
+            pltpu.VMEM((LAYER, 4 * width), F32),
+            pltpu.VMEM((12 * LAYER, lane_count), BF16),
+            pltpu.VMEM((12 * LAYER, 2 * width), F32),
             pltpu.VMEM((3 * LAYER, lane_count), BF16),
             pltpu.VMEM((2, 3 * LAYER, width), F32),
             pltpu.VMEM((nnz, blocks, width), jnp.int32),

time: 33.7 us -> 33.1 us (0.982)
  Pallas kernels: 32.7 us -> 32.1 us
    pallas_call x1, Pallas kernels: 32 us -> 31.3 us  [shards(): pl.pallas_call(functools.partial(force_kernel, blocks, width, nnz, peers)...]
where the time goes in v5:
time: 33.1 us; the launch traced here: 32.9 us
  Pallas kernels  32.1 us (97%)
  between operations  0.8 us (2%)
    pallas_call x1, Pallas kernels, shards(): pl.pallas_call(functools.partial(force_kernel, blocks, width, nnz, peers)...  31.3 us
    pallas_call x1, Pallas kernels, shards(): pl.pallas_call(store_kernel, out_shape=(shape, shape), in_specs=[pl.Block...  0.76 us

profile of v5, /device:TPU:5, one launch (start us, length us, event | category | flops | bytes accessed | tf_op | source)
XLA Modules:
  0.0 32.9 jit_solution(6693745369049390184)
XLA Ops:
  0.6 31.3 %forces.1 = (f32[128,3,128]{2,1,0:T(4,128)S(1)}, f32[128,3,128]{2,1,0:T(4,128)S(1)}) custom-call(s32[1,16,64]{2,1,0:T(8,128)} %send_hbm.1, s32[1,16,64]{2,1,0:T(8,128)} %arrive_hbm.1, s32[1,16]{1,0:T(1,128)} %count_hbm.1, s32[27,128]{1,0:T(8,128)} %bitcast.19, s32[27,128,128]{2,1,0:T(8,128)} %bitcast.15, f32[128,128]{1,0:T(8,128)} %bitcast.18, ...), custom_call_target="tpu_custom_call" | custom-call | tf_op jit(solution)/shard_map/forces/pallas_call | solution.py:635
  32.0 0.8 %store.1 = (f32[128,3,128]{2,1,0:T(4,128)}, f32[128,3,128]{2,1,0:T(4,128)}) custom-call(f32[128,3,128]{2,1,0:T(4,128)S(1)} %get-tuple-element.6.pos_in, f32[128,3,128]{2,1,0:T(4,128)S(1)} %get-tuple-element.7.vel_in), custom_call_target="tpu_custom_call" | custom-call | tf_op jit(solution)/shard_map/store/pallas_call | solution.py:699

commit v6 on v5

--- a/solution.py
+++ b/solution.py
@@ -347,12 +347,6 @@
         stiff = stiff + intact * totals
     stiff_ref[...] = stiff
 
-    for half in (0, 1):
-
-        @pl.when(exists(half))
-        def _():
-            index_copy(1 - half).wait_recv()
-
     def gain(ref, value):
         ref[...] = value if batches == 1 else ref[...] + value
 
@@ -371,8 +365,8 @@
             marks, node_ref[step, columns, :], (((1,), (1,)), ((), ())), preferred_element_type=F32
         )
 
-    def mark_batch(step):
-        for which in range(3):
+    def mark_batch(step, which_ones):
+        for which in which_ones:
             index = index_ref[which, step]
             inside = index & (width - 1)
             block = index >> shift
@@ -389,9 +383,15 @@
             block_ref[step, rows, :] = marks
             gain(hit_ref.at[:, columns], land(marks, columns, step))
 
-    clear([hit_ref])
-    each_batch(mark_batch)
-    clear([landed_ref, ghost_landed_ref])
+    clear([hit_ref, landed_ref, ghost_landed_ref])
+    each_batch(lambda step: mark_batch(step, (1,)))
+    for half in (0, 1):
+
+        @pl.when(exists(half))
+        def _():
+            index_copy(1 - half).wait_recv()
+
+    each_batch(lambda step: mark_batch(step, (0, 2)))
 
     for half in (0, 1):
         wait_halo(0, half, 0, lanes_of(0, 3))
@@ -518,8 +518,7 @@
         put(far, half, 0, soft_low)
         for row in range(3):
             put(far, half, 1 + row, (soft_wide * rounded[row]).astype(BF16))
-        for part, (first, rows) in enumerate(far_parts(parted)):
-            send(far, half, part, lanes_of(first, rows))
+        send(far, half, 0, lanes_of(0, 1))
         for row in range(3):
             stretch_ref[row, own(half), :] = stretch[row]
         soften_ref[own(half), :] = soften
@@ -529,9 +528,14 @@
         scaling = mod_ref[own(half), :]
         soften = soften_ref[own(half), :]
         kick = 0.5 * TIME_STEP if last else jnp.where(t == 0, 0.5 * TIME_STEP, TIME_STEP)
+        wait_halo(far, half, 0, lanes_of(0, 1))
+        ghost = pl.ds(pl.multiple_of(3 * LAYER * half, LAYER), LAYER)
+        soft_wide = ext_ref[far, ghost, lanes_of(0, 1)].astype(F32)
+        for row in range(3):
+            rounded = ext_ref[near, ghost, lanes_of(row, 1)].astype(F32)
+            ext_ref[far, ghost, lanes_of(1 + row, 1)] = (soft_wide * rounded).astype(BF16)
         paired = []
         for part, (first, rows) in enumerate(far_parts(parted)):
-            wait_halo(far, half, part, lanes_of(first, rows))
             begin = max(len(paired) - 1, 0)
             paired += contract(far, first, rows, half)
             for row in range(begin, len(paired) - 1):
@@ -582,7 +586,7 @@
     for row in range(3):
         pos_out[:, row, :] = pos_ref[row]
     pairing(SUBSTEPS, fast, False, True)
-    pairing(SUBSTEPS, slow, True, True)
+    pairing(SUBSTEPS, slow, False, True)
 
     pos_copy(0, 0, peers - 1).wait_send()
     vel_copy(0, 0, peers - 1).wait_send()
@@ -594,7 +598,7 @@
 
     for slot in range(1, slots):
         for half, parted in ((fast, False), (slow, True)):
-            parts = far_parts(parted) if slot % 2 else near_parts(parted)
+            parts = ((0, 1),) if slot % 2 else near_parts(parted)
             for part, (first, rows) in enumerate(parts):
                 wait_sent(slot, half, part, lanes_of(first, rows))
 

time: 33.1 us -> 32.6 us (0.985)
  Pallas kernels: 32.1 us -> 31.5 us
    pallas_call x1, Pallas kernels: 31.3 us -> 30.8 us  [shards(): pl.pallas_call(functools.partial(force_kernel, blocks, width, nnz, peers)...]
where the time goes in v6:
time: 32.6 us; the launch traced here: 32.3 us
  Pallas kernels  31.5 us (97%)
  between operations  0.8 us (2%)
    pallas_call x1, Pallas kernels, shards(): pl.pallas_call(functools.partial(force_kernel, blocks, width, nnz, peers)...  30.8 us
    pallas_call x1, Pallas kernels, shards(): pl.pallas_call(store_kernel, out_shape=(shape, shape), in_specs=[pl.Block...  0.76 us

profile of v6, /device:TPU:5, one launch (start us, length us, event | category | flops | bytes accessed | tf_op | source)
XLA Modules:
  0.0 32.3 jit_solution(16205440841600452505)
XLA Ops:
  0.6 30.8 %forces.1 = (f32[128,3,128]{2,1,0:T(4,128)S(1)}, f32[128,3,128]{2,1,0:T(4,128)S(1)}) custom-call(s32[1,16,64]{2,1,0:T(8,128)} %send_hbm.1, s32[1,16,64]{2,1,0:T(8,128)} %arrive_hbm.1, s32[1,16]{1,0:T(1,128)} %count_hbm.1, s32[27,128]{1,0:T(8,128)} %bitcast.19, s32[27,128,128]{2,1,0:T(8,128)} %bitcast.15, f32[128,128]{1,0:T(8,128)} %bitcast.18, ...), custom_call_target="tpu_custom_call" | custom-call | tf_op jit(solution)/shard_map/forces/pallas_call | solution.py:639
  31.4 0.8 %store.1 = (f32[128,3,128]{2,1,0:T(4,128)}, f32[128,3,128]{2,1,0:T(4,128)}) custom-call(f32[128,3,128]{2,1,0:T(4,128)S(1)} %get-tuple-element.6.pos_in, f32[128,3,128]{2,1,0:T(4,128)S(1)} %get-tuple-element.7.vel_in), custom_call_target="tpu_custom_call" | custom-call | tf_op jit(solution)/shard_map/store/pallas_call | solution.py:703

commit v7 on v6

--- a/solution.py
+++ b/solution.py
@@ -64,6 +64,7 @@
     onehot_ref,
     ext_ref,
     picked_ref,
+    soft_picked_ref,
     stiff_ref,
     stretch_ref,
     soften_ref,
@@ -303,7 +304,7 @@
         def _():
             index_ref[2 * half] = jnp.full(index_ref.shape[1:], nodes, jnp.int32)
             for slot in range(slots):
-                ext_ref[slot, pl.ds(3 * LAYER * half, LAYER), :] = jnp.zeros((LAYER, 4 * width), BF16)
+                ext_ref[slot, pl.ds(3 * LAYER * half, LAYER), :] = jnp.zeros((LAYER, 3 * width), BF16)
 
     for half in (0, 1):
         for row in range(3):
@@ -473,32 +474,37 @@
 
     group = 9 if nnz % 9 == 0 else nnz
 
-    def contract(slot, first, rows, half):
-        wide = rows * width
-        start = half * LAYER if isinstance(half, int) else pl.multiple_of(half * LAYER, LAYER)
+    def pick_blocks(slot, first, rows, half, target):
+        start = pl.multiple_of(half * LAYER, LAYER)
         source = ext_ref[slot, pl.ds(start, reach), lanes_of(first, rows)]
         for begin in range(0, nnz, group):
             part = pl.ds(begin * LAYER, group * LAYER)
-            picked_ref[part, lanes_of(first, rows)] = jnp.dot(
+            target[part, lanes_of(first, rows)] = jnp.dot(
                 onehot_ref[half, part, :], source, preferred_element_type=F32
             ).astype(BF16)
-        sums = [jnp.zeros((LAYER, width), F32) for _ in range(rows)]
+
+    def weigh(half, picks):
+        sums = [jnp.zeros((LAYER, width), F32) for _ in picks]
         for j in range(nnz):
             part = pl.ds(j * LAYER, LAYER)
             mask = intact_ref[j, own(half), :]
-            stacked = jnp.concatenate(
-                [picked_ref[part, lanes_of(first + row, 1)] for row in range(rows)], axis=0
-            )
+            stacked = jnp.concatenate([one(part) for one in picks], axis=0)
             product = jnp.dot(stacked, wt_ref[j], preferred_element_type=F32)
-            for row in range(rows):
-                sums[row] = sums[row] + product[row * LAYER : (row + 1) * LAYER] * mask
+            for i in range(len(picks)):
+                sums[i] = sums[i] + product[i * LAYER : (i + 1) * LAYER] * mask
         return sums
+
+    def placed(half, row):
+        return lambda part: picked_ref[half, part, lanes_of(row, 1)]
+
+    def softened(half, row):
+        return lambda part: picked_ref[half, part, lanes_of(row, 1)] * soft_picked_ref[part, :]
+
+    def softening(part):
+        return soft_picked_ref[part, :]
 
     def near_parts(parted):
         return ((0, 1), (1, 2)) if parted else ((0, 3),)
-
-    def far_parts(parted):
-        return ((0, 2), (2, 2)) if parted else ((0, 4),)
 
     def stretching(t, half, parted, waits):
         near, far = 2 * t, 2 * t + 1
@@ -506,7 +512,8 @@
         for part, (first, rows) in enumerate(near_parts(parted and waits)):
             if waits:
                 wait_halo(near, half, part, lanes_of(first, rows))
-            summed += contract(near, first, rows, half)
+            pick_blocks(near, first, rows, half, picked_ref.at[half])
+            summed += weigh(half, [placed(half, first + row) for row in range(rows)])
         scaling = mod_ref[own(half), :]
         stiffness = stiff_ref[own(half), :]
         rounded = [get(near, half, row) for row in range(3)]
@@ -514,10 +521,7 @@
         dilatation = (stretch[0] + stretch[1] + stretch[2]) / 3.0
         soften = 1.0 / (1.0 + dilatation * dilatation)
         soft_low = soften.astype(BF16)
-        soft_wide = soft_low.astype(F32)
         put(far, half, 0, soft_low)
-        for row in range(3):
-            put(far, half, 1 + row, (soft_wide * rounded[row]).astype(BF16))
         send(far, half, 0, lanes_of(0, 1))
         for row in range(3):
             stretch_ref[row, own(half), :] = stretch[row]
@@ -529,19 +533,17 @@
         soften = soften_ref[own(half), :]
         kick = 0.5 * TIME_STEP if last else jnp.where(t == 0, 0.5 * TIME_STEP, TIME_STEP)
         wait_halo(far, half, 0, lanes_of(0, 1))
-        ghost = pl.ds(pl.multiple_of(3 * LAYER * half, LAYER), LAYER)
-        soft_wide = ext_ref[far, ghost, lanes_of(0, 1)].astype(F32)
-        for row in range(3):
-            rounded = ext_ref[near, ghost, lanes_of(row, 1)].astype(F32)
-            ext_ref[far, ghost, lanes_of(1 + row, 1)] = (soft_wide * rounded).astype(BF16)
-        paired = []
-        for part, (first, rows) in enumerate(far_parts(parted)):
-            begin = max(len(paired) - 1, 0)
-            paired += contract(far, first, rows, half)
-            for row in range(begin, len(paired) - 1):
+        pick_blocks(far, 0, 1, half, soft_picked_ref)
+        for part, (first, rows) in enumerate(near_parts(parted)):
+            picks = [softened(half, first + row) for row in range(rows)]
+            if part == 0:
+                soft_sum, *paired = weigh(half, [softening] + picks)
+            else:
+                paired = weigh(half, picks)
+            for row in range(first, first + rows):
                 rounded = get(near, half, row)
                 force = 0.5 * (
-                    scaling * (paired[1 + row] - rounded * paired[0]) + soften * stretch_ref[row, own(half), :]
+                    scaling * (paired[row - first] - rounded * soft_sum) + soften * stretch_ref[row, own(half), :]
                 )
                 speed = vel_ref[row, own(half), :] + kick * force
                 if last:
@@ -552,7 +554,7 @@
                     pos_ref[row, own(half), :] = moved
                     put(near + 2, half, row, moved.astype(BF16))
             if not last:
-                send(near + 2, half, part, lanes_of(*near_parts(parted)[part]))
+                send(near + 2, half, part, lanes_of(first, rows))
 
     stretching(0, slow, True, False)
 
@@ -670,8 +672,9 @@
             pltpu.VMEM((nnz, blocks, width), F32),
             pltpu.VMEM((nnz, width, width), BF16),
             pltpu.VMEM((2, nnz * LAYER, 3 * LAYER), BF16),
-            pltpu.VMEM((slots, 4 * LAYER, 4 * width), BF16),
-            pltpu.VMEM((nnz * LAYER, 4 * width), BF16),
+            pltpu.VMEM((slots, 4 * LAYER, 3 * width), BF16),
+            pltpu.VMEM((2, nnz * LAYER, 3 * width), BF16),
+            pltpu.VMEM((nnz * LAYER, width), BF16),
             pltpu.VMEM((blocks, width), F32),
             pltpu.VMEM((3, blocks, width), F32),
             pltpu.VMEM((blocks, width), F32),

time: 32.6 us -> 31.9 us (0.979)
  Pallas kernels: 31.5 us -> 30.8 us
    pallas_call x1, Pallas kernels: 30.8 us -> 30.1 us  [shards(): pl.pallas_call(functools.partial(force_kernel, blocks, width, nnz, peers)...]
where the time goes in v7:
time: 31.9 us; the launch traced here: 31.6 us
  Pallas kernels  30.8 us (97%)
  between operations  0.8 us (3%)
    pallas_call x1, Pallas kernels, shards(): pl.pallas_call(functools.partial(force_kernel, blocks, width, nnz, peers)...  30.1 us
    pallas_call x1, Pallas kernels, shards(): pl.pallas_call(store_kernel, out_shape=(shape, shape), in_specs=[pl.Block...  0.76 us

profile of v7, /device:TPU:5, one launch (start us, length us, event | category | flops | bytes accessed | tf_op | source)
XLA Modules:
  0.0 31.6 jit_solution(6662752511169948663)
XLA Ops:
  0.6 30.1 %forces.1 = (f32[128,3,128]{2,1,0:T(4,128)S(1)}, f32[128,3,128]{2,1,0:T(4,128)S(1)}) custom-call(s32[1,16,64]{2,1,0:T(8,128)} %send_hbm.1, s32[1,16,64]{2,1,0:T(8,128)} %arrive_hbm.1, s32[1,16]{1,0:T(1,128)} %count_hbm.1, s32[27,128]{1,0:T(8,128)} %bitcast.19, s32[27,128,128]{2,1,0:T(8,128)} %bitcast.15, f32[128,128]{1,0:T(8,128)} %bitcast.18, ...), custom_call_target="tpu_custom_call" | custom-call | tf_op jit(solution)/shard_map/forces/pallas_call | solution.py:641
  30.7 0.8 %store.1 = (f32[128,3,128]{2,1,0:T(4,128)}, f32[128,3,128]{2,1,0:T(4,128)}) custom-call(f32[128,3,128]{2,1,0:T(4,128)S(1)} %get-tuple-element.6.pos_in, f32[128,3,128]{2,1,0:T(4,128)S(1)} %get-tuple-element.7.vel_in), custom_call_target="tpu_custom_call" | custom-call | tf_op jit(solution)/shard_map/store/pallas_call | solution.py:706

commit v8 on v7

--- a/solution.py
+++ b/solution.py
@@ -286,14 +286,10 @@
         pos_in[row] = pos_raw[:, row, :]
     each_batch(gather_places)
     in_pos[me, 0:6, :] = out_pos[me + 1, 0:6, :]
+    for half in (0, 1):
+        for row in range(3):
+            put(0, half, row, pos_in[row, own(half), :].astype(BF16))
     pl.semaphore_wait(barrier, peers - 1)
-
-    def start_places(step, carry):
-        pos_copy(lax.rem(me + step, count) + 1, me).start()
-        return carry
-
-    lax.fori_loop(1, peers, start_places, 0)
-
     for half in (0, 1):
 
         @pl.when(exists(half))
@@ -307,16 +303,22 @@
                 ext_ref[slot, pl.ds(3 * LAYER * half, LAYER), :] = jnp.zeros((LAYER, 3 * width), BF16)
 
     for half in (0, 1):
-        for row in range(3):
-            put(0, half, row, pos_in[row, own(half), :].astype(BF16))
         send(0, half, 0, lanes_of(0, 3))
+
+
+    def start_places(step, carry):
+        pos_copy(lax.rem(me + step, count) + 1, me).start()
+        return carry
+
+    lax.fori_loop(1, peers, start_places, 0)
 
     lanes = lax.broadcasted_iota(jnp.int32, (LAYER, reach), 1)
     fetches["hor"].wait()
     padding = jnp.zeros((-nnz % 8, blocks), jnp.int32)
     horizon = jnp.transpose(jnp.concatenate([hor_ref[...], padding], axis=0))
     for half in range(2):
-        local = horizon[half * LAYER : (half + 1) * LAYER] - (me * blocks - LAYER + half * LAYER)
+        local = horizon[half * LAYER : (half + 1) * LAYER] - me * blocks
+        local = jnp.where(local < 0, local + reach, local)
         for j in range(nnz):
             hit = local[:, j : j + 1] == lanes
             onehot_ref[half, pl.ds(j * LAYER, LAYER), :] = jnp.where(hit, 1.0, 0.0).astype(BF16)
@@ -474,13 +476,34 @@
 
     group = 9 if nnz % 9 == 0 else nnz
 
+    def ghost_of(half):
+        return pl.ds(pl.multiple_of(3 * LAYER * half, LAYER), LAYER)
+
     def pick_blocks(slot, first, rows, half, target):
-        start = pl.multiple_of(half * LAYER, LAYER)
-        source = ext_ref[slot, pl.ds(start, reach), lanes_of(first, rows)]
+        columns = lanes_of(first, rows)
+        source = jnp.concatenate(
+            [ext_ref[slot, pl.ds(LAYER, 2 * LAYER), columns], ext_ref[slot, ghost_of(half), columns]], axis=0
+        )
         for begin in range(0, nnz, group):
             part = pl.ds(begin * LAYER, group * LAYER)
-            target[part, lanes_of(first, rows)] = jnp.dot(
+            target[part, columns] = jnp.dot(
                 onehot_ref[half, part, :], source, preferred_element_type=F32
+            ).astype(BF16)
+
+    def pick_own(slot, half, target):
+        source = ext_ref[slot, pl.ds(LAYER, 2 * LAYER), lanes_of(0, 1)]
+        for begin in range(0, nnz, group):
+            part = pl.ds(begin * LAYER, group * LAYER)
+            target[part, lanes_of(0, 1)] = jnp.dot(
+                onehot_ref[half, part, 0 : 2 * LAYER], source, preferred_element_type=F32
+            ).astype(BF16)
+
+    def pick_ghost(slot, half, target):
+        source = ext_ref[slot, ghost_of(half), lanes_of(0, 1)]
+        for begin in range(0, nnz, group):
+            part = pl.ds(begin * LAYER, group * LAYER)
+            target[part, lanes_of(0, 1)] = target[part, lanes_of(0, 1)] + jnp.dot(
+                onehot_ref[half, part, 2 * LAYER : reach], source, preferred_element_type=F32
             ).astype(BF16)
 
     def weigh(half, picks):
@@ -510,9 +533,15 @@
         near, far = 2 * t, 2 * t + 1
         summed = []
         for part, (first, rows) in enumerate(near_parts(parted and waits)):
+            single = waits and rows == 1
+            if single:
+                pick_own(near, half, picked_ref.at[half])
             if waits:
                 wait_halo(near, half, part, lanes_of(first, rows))
-            pick_blocks(near, first, rows, half, picked_ref.at[half])
+            if single:
+                pick_ghost(near, half, picked_ref.at[half])
+            else:
+                pick_blocks(near, first, rows, half, picked_ref.at[half])
             summed += weigh(half, [placed(half, first + row) for row in range(rows)])
         scaling = mod_ref[own(half), :]
         stiffness = stiff_ref[own(half), :]

time: 31.9 us -> 31.9 us (level)
  no operation moved by 1% of the time
where the time goes in v8:
time: 31.9 us; the launch traced here: 31.7 us
  Pallas kernels  30.9 us (97%)
  between operations  0.8 us (3%)
    pallas_call x1, Pallas kernels, shards(): pl.pallas_call(functools.partial(force_kernel, blocks, width, nnz, peers)...  30.1 us
    pallas_call x1, Pallas kernels, shards(): pl.pallas_call(store_kernel, out_shape=(shape, shape), in_specs=[pl.Block...  0.76 us

profile of v8, /device:TPU:5, one launch (start us, length us, event | category | flops | bytes accessed | tf_op | source)
XLA Modules:
  0.0 31.7 jit_solution(6059865980310006343)
XLA Ops:
  0.6 30.1 %forces.1 = (f32[128,3,128]{2,1,0:T(4,128)S(1)}, f32[128,3,128]{2,1,0:T(4,128)S(1)}) custom-call(s32[1,16,64]{2,1,0:T(8,128)} %send_hbm.1, s32[1,16,64]{2,1,0:T(8,128)} %arrive_hbm.1, s32[1,16]{1,0:T(1,128)} %count_hbm.1, s32[27,128]{1,0:T(8,128)} %bitcast.19, s32[27,128,128]{2,1,0:T(8,128)} %bitcast.15, f32[128,128]{1,0:T(8,128)} %bitcast.18, ...), custom_call_target="tpu_custom_call" | custom-call | tf_op jit(solution)/shard_map/forces/pallas_call | solution.py:670
  30.7 0.8 %store.1 = (f32[128,3,128]{2,1,0:T(4,128)}, f32[128,3,128]{2,1,0:T(4,128)}) custom-call(f32[128,3,128]{2,1,0:T(4,128)S(1)} %get-tuple-element.6.pos_in, f32[128,3,128]{2,1,0:T(4,128)S(1)} %get-tuple-element.7.vel_in), custom_call_target="tpu_custom_call" | custom-call | tf_op jit(solution)/shard_map/store/pallas_call | solution.py:735

commit v9 on v8

--- a/solution.py
+++ b/solution.py
@@ -474,7 +474,7 @@
                 landed = landed_ref[pl.ds(row * LAYER, LAYER), own_columns(half)]
                 put(0, half, row, jnp.where(hit, landed, get(0, half, row)).astype(BF16))
 
-    group = 9 if nnz % 9 == 0 else nnz
+    group = 3 if nnz % 3 == 0 else nnz
 
     def ghost_of(half):
         return pl.ds(pl.multiple_of(3 * LAYER * half, LAYER), LAYER)

time: 31.9 us -> 31.6 us (level)
  no operation moved by 1% of the time
where the time goes in v9:
time: 31.6 us; the launch traced here: 31.4 us
  Pallas kernels  30.6 us (97%)
  between operations  0.8 us (3%)
    pallas_call x1, Pallas kernels, shards(): pl.pallas_call(functools.partial(force_kernel, blocks, width, nnz, peers)...  29.9 us
    pallas_call x1, Pallas kernels, shards(): pl.pallas_call(store_kernel, out_shape=(shape, shape), in_specs=[pl.Block...  0.76 us

profile of v9, /device:TPU:5, one launch (start us, length us, event | category | flops | bytes accessed | tf_op | source)
XLA Modules:
  0.0 31.4 jit_solution(2579657599330498784)
XLA Ops:
  0.6 29.9 %forces.1 = (f32[128,3,128]{2,1,0:T(4,128)S(1)}, f32[128,3,128]{2,1,0:T(4,128)S(1)}) custom-call(s32[1,16,64]{2,1,0:T(8,128)} %send_hbm.1, s32[1,16,64]{2,1,0:T(8,128)} %arrive_hbm.1, s32[1,16]{1,0:T(1,128)} %count_hbm.1, s32[27,128]{1,0:T(8,128)} %bitcast.19, s32[27,128,128]{2,1,0:T(8,128)} %bitcast.15, f32[128,128]{1,0:T(8,128)} %bitcast.18, ...), custom_call_target="tpu_custom_call" | custom-call | tf_op jit(solution)/shard_map/forces/pallas_call | solution.py:670
  30.5 0.8 %store.1 = (f32[128,3,128]{2,1,0:T(4,128)}, f32[128,3,128]{2,1,0:T(4,128)}) custom-call(f32[128,3,128]{2,1,0:T(4,128)S(1)} %get-tuple-element.6.pos_in, f32[128,3,128]{2,1,0:T(4,128)S(1)} %get-tuple-element.7.vel_in), custom_call_target="tpu_custom_call" | custom-call | tf_op jit(solution)/shard_map/store/pallas_call | solution.py:735
